TPU v7x, 32 devices: a whole 2x2x4 slice. The times are simulated.
32 devices in a mesh: band: 4 (over y, x), pair: 8 (over z, core).
Axes of the slice: x: 2, y: 2, z: 4, core: 2. Of those that a mesh axis runs over, the one named last changes fastest.
Arguments:
- visibilities: float32 [4, 16, 8, 2, 1024], P('band', 'pair'), may hold values from -6 to 6
- coherencies: bfloat16 [4, 16, 8, 2, 32, 1024], P('band', 'pair'), may hold values from -1 to 1
- block_tiles: int32 [16, 2], P('pair'), may hold values from 0 to 15, as said below
- sample_counts: int32 [16], P('pair'), may hold values from 1 to 8, as said below
- gains: float32 [4, 2, 32, 512], P('band', None, None, 'pair'), may hold values from 0.5 to 1.5
- targets: float32 [4, 2, 32, 512], P('band', None, None, 'pair'), may hold values from 0.5 to 1.5
- multipliers: float32 [4, 2, 32, 512], P('band', None, None, 'pair'), may hold values from -2 to 2
Outputs:
- new_gains: float32 [4, 2, 32, 512], P('band', None, None, 'pair')
- new_targets: float32 [4, 2, 32, 512], P('band', None, None, 'pair')
- new_multipliers: float32 [4, 2, 32, 512], P('band', None, None, 'pair')
Inputs may be any that keep to these rules, and one draw needn't show every extreme that they name: `block_tiles`: each row names two station tiles a <= b; no tile pair appears twice; the pairs (0, 15) and (15, 15) are always among them. `sample_counts`: some block has all 8 samples and some block only one.
All inputs are finite; a program needn't handle non-finite values.
Results may differ from a plain program's by a relative error of at most 0.0003.
Values sent between devices are 32-bit elements; how exact they have to be, the bound alone decides.
No kernel may reach another device: no remote copies, remote signals or barrier semaphores. Data moves between devices by JAX's collectives and lax.ppermute only.
A program may use at most 64 MiB of HBM per device.

v0:
```python
import math

import jax
import jax.numpy as jnp
import numpy as np
from jax import lax
from jax.experimental import pallas as pl
from jax.experimental.pallas import tpu as pltpu
from jax.sharding import PartitionSpec as P


P_SIZE = 8
TILE = 32
LANES = 128
GROUP = LANES // TILE

ridge = 0.05
penalty = 0.25


def fit_matrix(freq_count, term_count):
    positions = (np.arange(freq_count) + 0.5) / freq_count
    basis = np.stack(
        [
            math.comb(term_count - 1, degree)
            * positions**degree
            * (1.0 - positions) ** (term_count - 1 - degree)
            for degree in range(term_count)
        ],
        axis=1,
    )
    normal = basis.T @ basis + ridge * np.eye(term_count)
    factor = np.linalg.cholesky(normal)
    half = np.linalg.solve(factor, basis.T)
    return half.T @ half


class Plan:
    def __init__(self, directions, stations, pairs, blocks, times, cells):
        self.k = directions
        self.sl = stations
        self.zn = pairs // 2
        self.blocks = blocks
        self.times = times
        self.cells = cells
        self.steps = cells // LANES
        self.per = stations // TILE
        self.parts = 1 if self.per else TILE // stations
        self.rows = 2 * directions + 8 * ((blocks + 7) // 8)
        assert 2 * stations <= LANES and directions == 32 and times <= 8 and self.steps == 8

    def lane(self, rows=None):
        return lax.broadcasted_iota(jnp.int32, (self.k if rows is None else rows, LANES), 1)

    def owner(self, me, device):
        return (device % 2) == (me % 2), (device // 2) ^ (me // 2)

    def record(self, me, own_ref, sib_ref, device, row):
        same, slot = self.owner(me, device)
        own = own_ref[slot, row : row + self.k, :]
        sib = sib_ref[slot, row : row + self.k, :]
        return jnp.where(same, own, sib)

    def fetch(self, me, own_ref, sib_ref, tile, row):
        lane = self.lane()
        part, spot = lane // TILE % 2, lane % TILE
        if self.per:
            device = tile // self.per
            sub = tile - device * self.per
            rec = self.record(me, own_ref, sib_ref, device, row)
            return take(rec, part * self.sl + sub * TILE + spot)
        value = None
        for r in range(self.parts):
            rec = self.record(me, own_ref, sib_ref, tile * self.parts + r, row)
            here = take(rec, part * self.sl + spot % self.sl)
            value = here if value is None else jnp.where(spot // self.sl == r, here, value)
        return value

    def place(self, terms, shift, sub):
        lane = self.lane()
        part, spot = lane // self.sl % 2, lane % self.sl
        if self.per:
            value = take(terms, shift + part * TILE + spot % TILE)
            keep = spot // TILE == sub
        else:
            value = take(terms, shift + part * TILE + sub * self.sl + spot)
            keep = lane < 2 * self.sl
        return jnp.where(keep, value, 0.0)

    def spread(self, me, tile, terms, shift, own_ref, sib_ref):
        if self.per:
            device = tile // self.per
            spots = [(device, tile - device * self.per)]
        else:
            spots = [(tile * self.parts + r, r) for r in range(self.parts)]
        for device, sub in spots:
            value = self.place(terms, shift, sub)
            same, slot = self.owner(me, device)
            own_ref[slot] = own_ref[slot] + jnp.where(same, value, 0.0)
            sib_ref[slot] = sib_ref[slot] + jnp.where(same, 0.0, value)

    def record_of(self, raw_ref):
        pieces = [raw_ref[0, 0], raw_ref[0, 1]]
        if 2 * self.sl < LANES:
            pieces.append(jnp.zeros((self.k, LANES - 2 * self.sl), jnp.float32))
        return jnp.concatenate(pieces, axis=1)


def take(value, lanes):
    return jnp.take_along_axis(value, lanes, axis=1, mode="promise_in_bounds")


def merge(low, first, second, shift, axis):
    size = first.shape[axis]
    if 2 * shift == size:
        mixed = jnp.where(low, second, first)
        return jnp.where(low, first, second) + pltpu.roll(mixed, shift, axis)
    up = first + pltpu.roll(first, size - shift, axis)
    down = second + pltpu.roll(second, shift, axis)
    return jnp.where(low, up, down)


def merge_all(items, shifts, axis):
    index = lax.broadcasted_iota(jnp.int32, items[0].shape, axis)
    for shift in shifts:
        half = len(items) // 2
        low = (index & shift) == 0
        items = [merge(low, items[i], items[i + half], shift, axis) for i in range(half)]
    return items


def eights(value):
    return [value[8 * i : 8 * i + 8] for i in range(value.shape[0] // 8)]


def pack_kernel(plan, tiles_hbm, counts_hbm, gains_hbm, targets_hbm, mult_hbm, out_ref, meta_ref, mrec_ref, *scratch):
    bufs, sems = scratch[:-1], scratch[-1]
    copies = [
        pltpu.make_async_copy(src, dst, sems.at[i])
        for i, (src, dst) in enumerate(zip((gains_hbm, targets_hbm, mult_hbm, tiles_hbm, counts_hbm), bufs))
    ]
    for copy in copies:
        copy.start()
    for copy in copies:
        copy.wait()
    gains_ref, targets_ref, mult_ref, tiles_ref, counts_ref = bufs
    k = plan.k
    gain = plan.record_of(gains_ref)
    target = plan.record_of(targets_ref)
    mult = plan.record_of(mult_ref)
    out_ref[:k] = gain
    out_ref[k : 2 * k] = gain - penalty * (gain - target + mult)
    mrec_ref[...] = mult
    lane = plan.lane(8)
    sub = lax.broadcasted_iota(jnp.int32, (8, LANES), 0)
    meta = jnp.zeros((8, LANES), jnp.int32)
    for base in range(0, plan.blocks, 8):
        rows = jnp.zeros((8, LANES), jnp.int32)
        for n in range(base, min(base + 8, plan.blocks)):
            ids = jnp.where(lane < 2 * TILE, tiles_ref[n, 0], tiles_ref[n, 1])
            rows = jnp.where(sub == n - base, ids, rows)
            for j, number in enumerate((tiles_ref[n, 0], tiles_ref[n, 1], counts_ref[n])):
                meta = jnp.where(lane == 3 * n + j, number, meta)
        out_ref[2 * k + base : 2 * k + base + 8] = rows.astype(jnp.float32)
    meta_ref[...] = meta


def load_kernel(plan, vis_hbm, coh_hbm, vis_ref, coh_ref, vis_buf, coh_buf, sems):
    halves = 2
    cells = plan.cells // halves
    copies = []
    for n in range(plan.blocks):
        for h in range(halves):
            lanes = pl.ds(h * cells, cells)
            copies.append(
                pltpu.make_async_copy(
                    coh_hbm.at[0, n, :, :, :, lanes],
                    coh_buf.at[n, :, :, :, lanes],
                    sems.at[n * halves + h],
                )
            )
    last = pltpu.make_async_copy(vis_hbm.at[0], vis_buf, sems.at[plan.blocks * halves])
    for copy in copies:
        copy.start()
    last.start()
    for n in range(plan.blocks):
        for h in range(halves):
            copies[n * halves + h].wait()

            def convert(t, carry, n=n, h=h):
                lanes = pl.ds(h * cells, cells)
                coh_ref[n, t, :, :, lanes] = coh_buf[n, t, :, :, lanes].astype(jnp.float32)
                return carry

            lax.fori_loop(0, plan.times, convert, 0)
    last.wait()
    for n in range(plan.blocks):
        for part in range(2):
            vis_ref[n, part] = vis_buf[n, :, part, :]


def block_gradients(plan, meta_ref, tile_gains, vis_ref, coh_ref, right_ref, left_ref, second_ref, first_ref):
    k, times, steps = plan.k, plan.times, plan.steps
    lane_k = plan.lane()
    lane = plan.lane(8)
    sample = lax.broadcasted_iota(jnp.int32, (8, LANES), 0)
    for n, (left, right) in enumerate(tile_gains):
        left_ref[n] = left
        right_ref[n, 0] = take(right, lane_k % TILE)
        right_ref[n, 1] = take(right, TILE + lane_k % TILE)
        second_ref[n] = jnp.zeros((2, k, LANES), jnp.float32)

    def lefts(n, index):
        left = left_ref[n]
        spot = index * GROUP + lane_k // TILE
        return take(left, spot), take(left, TILE + spot)

    def where_is(q):
        n = q // steps
        index = q - n * steps
        return n, index, pl.ds(pl.multiple_of(index * LANES, LANES), LANES)

    def residual(q):
        n, index, lanes = where_is(q)
        lr, li = lefts(n, index)
        rr, ri = right_ref[n, 0], right_ref[n, 1]
        pr = lr * rr + li * ri
        pi = li * rr - lr * ri
        reals, imags = [], []
        for t in range(times):
            cr = coh_ref[n, t, 0, :, lanes]
            ci = coh_ref[n, t, 1, :, lanes]
            reals.append(sum(eights(pr * cr - pi * ci)))
            imags.append(sum(eights(pr * ci + pi * cr)))
        none = jnp.zeros((8, LANES), jnp.float32)
        reals += [none] * (8 - times)
        imags += [none] * (8 - times)
        (mr,) = merge_all(reals, (4, 2, 1), 0)
        (mi,) = merge_all(imags, (4, 2, 1), 0)
        upper = index * GROUP + lane // TILE - lane % TILE
        differ = meta_ref[0, 3 * n] != meta_ref[0, 3 * n + 1]
        bound = jnp.where(differ, steps * LANES, 0)
        keep = (upper < bound) & (sample < meta_ref[0, 3 * n + 2])
        er = jnp.where(keep, vis_ref[n, 0, :, lanes] - mr, 0.0)
        ei = jnp.where(keep, vis_ref[n, 1, :, lanes] - mi, 0.0)
        return er, ei

    def gradient(q, errors):
        er, ei = errors
        n, index, lanes = where_is(q)
        acc_re = acc_im = None
        for t in range(times):
            cr = coh_ref[n, t, 0, :, lanes]
            ci = coh_ref[n, t, 1, :, lanes]
            r = jnp.broadcast_to(er[t : t + 1], (k, LANES))
            i = jnp.broadcast_to(ei[t : t + 1], (k, LANES))
            re = r * cr + i * ci
            im = i * cr - r * ci
            acc_re = re if acc_re is None else acc_re + re
            acc_im = im if acc_im is None else acc_im + im
        lr, li = lefts(n, index)
        rr, ri = right_ref[n, 0], right_ref[n, 1]
        second_ref[n, 0] = second_ref[n, 0] + (acc_re * lr + acc_im * li)
        second_ref[n, 1] = second_ref[n, 1] + (acc_re * li - acc_im * lr)
        parts = eights(acc_re * rr - acc_im * ri) + eights(acc_re * ri + acc_im * rr)
        (total,) = merge_all(parts, (16, 8, 4), 1)
        for shift in (2, 1):
            (total,) = merge_all([total, total], (shift,), 1)
        first_ref[n, index] = total

    def step(q, errors):
        following = residual(q + 1)
        gradient(q, errors)
        return following

    final = plan.blocks * steps - 1
    gradient(final, lax.fori_loop(0, final, step, residual(0)))

    results = []
    for n in range(plan.blocks):
        packed = []
        for base in range(0, steps, 4):
            value = first_ref[n, base]
            for r in range(1, 4):
                value = jnp.where(lane % 4 == r, first_ref[n, base + r], value)
            packed.append(value)
        seconds = merge_all(eights(second_ref[n, 0]) + eights(second_ref[n, 1]), (64, 32), 1)
        part, spot = lane // TILE % 2, lane % TILE
        rows = []
        for group in range(k // 8):
            source = spot % GROUP * TILE + part * 16 + group * 4 + spot // GROUP % 4
            value = take(packed[0], source)
            for h in range(1, len(packed)):
                value = jnp.where(spot // 16 == h, take(packed[h], source), value)
            other = take(seconds[group % 2], part * 64 + group // 2 * TILE + spot)
            rows.append(jnp.where(lane < 2 * TILE, value, other))
        results.append(jnp.concatenate(rows, axis=0))
    return results


def first_kernel(plan, meta_ref, own_ref, sib_ref, vis_ref, coh_ref, out_ref, *scratch):
    me = lax.axis_index("pair")
    tile_gains = [
        [plan.fetch(me, own_ref, sib_ref, meta_ref[0, 3 * n + side], 0) for side in range(2)]
        for n in range(plan.blocks)
    ]
    for n, terms in enumerate(block_gradients(plan, meta_ref, tile_gains, vis_ref, coh_ref, *scratch)):
        out_ref[n] = terms


def second_kernel(
    plan, step_size, meta_ref, own_ref, sib_ref, term_own_ref, term_sib_ref, mult_ref, vis_ref, coh_ref,
    part_own_ref, part_sib_ref, rest_ref, *scratch,
):
    k = plan.k
    me = lax.axis_index("pair")
    wanted = [meta_ref[0, 3 * n + side] for n in range(plan.blocks) for side in range(2)]
    if plan.per:
        wanted += [me * plan.per + s for s in range(plan.per)]
    else:
        wanted += [me // plan.parts]
    labels = [t.astype(jnp.float32) for t in wanted]

    def gather(slot, sums):
        for pay_ref, term_ref in ((own_ref, term_own_ref), (sib_ref, term_sib_ref)):
            ids_all = pay_ref[slot, 2 * k : plan.rows, :]
            for n in range(plan.blocks):
                ids = ids_all[n : n + 1]
                terms = term_ref[slot, n]
                sums = [s + jnp.where(ids == label, terms, 0.0) for s, label in zip(sums, labels)]
        return sums

    sums = [jnp.zeros((k, LANES), jnp.float32) for _ in wanted]
    if plan.zn <= 4:
        for slot in range(plan.zn):
            sums = gather(slot, sums)
    else:
        sums = lax.fori_loop(0, plan.zn, gather, sums)
    sums = [s + pltpu.roll(s, LANES // 2, 1) for s in sums]

    tile_gains = [
        [
            plan.fetch(me, own_ref, sib_ref, wanted[2 * n + side], k) + step_size * sums[2 * n + side]
            for side in range(2)
        ]
        for n in range(plan.blocks)
    ]

    mine = sums[2 * plan.blocks :]
    if plan.per:
        own_sum = sum(plan.place(value, 0, s) for s, value in enumerate(mine))
    else:
        own_sum = plan.place(mine[0], 0, me % plan.parts)
    start = own_ref[0, :k, :]
    base = own_ref[0, k : 2 * k, :]
    pull = base - (1.0 - penalty) * start
    rest = (1.0 - penalty) * (base + step_size * own_sum) + pull
    rest_ref[0] = rest
    rest_ref[1] = rest + mult_ref[...]

    part_own_ref[...] = jnp.zeros_like(part_own_ref)
    part_sib_ref[...] = jnp.zeros_like(part_sib_ref)
    for n, terms in enumerate(block_gradients(plan, meta_ref, tile_gains, vis_ref, coh_ref, *scratch)):
        for side in range(2):
            plan.spread(me, meta_ref[0, 3 * n + side], terms, side * 2 * TILE, part_own_ref, part_sib_ref)


def fit_kernel(plan, fit, gain_ref, own_ref, *refs):
    others, (gain_out, target_out, mult_out) = refs[:-3], refs[-3:]
    sl = plan.sl
    band = lax.axis_index("band")
    total = None
    for m, ref in enumerate((own_ref,) + tuple(others)):
        factor = jnp.float32(0.0)
        for f in range(fit.shape[0]):
            factor = jnp.where(band == f, jnp.float32(fit[f, f ^ m]), factor)
        value = factor * ref[...]
        total = value if total is None else total + value
    change = own_ref[...] - total
    gain = gain_ref[...]
    for part in range(2):
        lanes = slice(part * sl, (part + 1) * sl)
        gain_out[0, part] = gain[:, lanes]
        target_out[0, part] = total[:, lanes]
        mult_out[0, part] = change[:, lanes]


def exchange(value, axis, size, mask):
    return lax.ppermute(value, axis, [(i, i ^ mask) for i in range(size)])


def local(visibilities, coherencies, block_tiles, sample_counts, gains, targets, multipliers):
    pairs = lax.axis_size("pair")
    bands = lax.axis_size("band")
    _, blocks, times, _, directions, cells = coherencies.shape
    stations = gains.shape[3]
    plan = Plan(directions, stations, pairs, blocks, times, cells)
    k, zn = plan.k, plan.zn
    tile_count = stations * pairs // TILE
    step_size = 0.25 * tile_count * k / (times * TILE * blocks * pairs)

    smem = pl.BlockSpec(memory_space=pltpu.SMEM)
    vmem = pl.BlockSpec(memory_space=pltpu.VMEM)
    hbm = pl.BlockSpec(memory_space=pltpu.HBM)
    stay = lambda value: pltpu.with_memory_space_constraint(value, pltpu.HBM)
    f32 = lambda *shape: jax.ShapeDtypeStruct(shape, jnp.float32)
    scratch = [
        pltpu.VMEM((blocks, 2, k, LANES), jnp.float32),
        pltpu.VMEM((blocks, k, LANES), jnp.float32),
        pltpu.VMEM((blocks, 2, k, LANES), jnp.float32),
        pltpu.VMEM((blocks, plan.steps, 8, LANES), jnp.float32),
    ]
    params = pltpu.CompilerParams(vmem_limit_bytes=16 << 20)

    payload, meta, mult_rec = pl.pallas_call(
        lambda *refs: pack_kernel(plan, *refs),
        name="pack",
        in_specs=[hbm] * 5,
        out_specs=[vmem] * 3,
        out_shape=[f32(plan.rows, LANES), jax.ShapeDtypeStruct((8, LANES), jnp.int32), f32(k, LANES)],
        scratch_shapes=[pltpu.VMEM(gains.shape, jnp.float32)] * 3
        + [
            pltpu.SMEM(block_tiles.shape, jnp.int32),
            pltpu.SMEM(sample_counts.shape, jnp.int32),
            pltpu.SemaphoreType.DMA((5,)),
        ],
        compiler_params=params,
    )(*map(stay, (block_tiles, sample_counts, gains, targets, multipliers)))

    vis, coh = pl.pallas_call(
        lambda *refs: load_kernel(plan, *refs),
        name="load",
        in_specs=[hbm] * 2,
        out_specs=[vmem] * 2,
        out_shape=[f32(blocks, 2, times, cells), f32(blocks, times, 2, k, cells)],
        scratch_shapes=[
            pltpu.VMEM((blocks, times, 2, cells), jnp.float32),
            pltpu.VMEM((blocks, times, 2, k, cells), jnp.bfloat16),
            pltpu.SemaphoreType.DMA((2 * blocks + 1,)),
        ],
        compiler_params=params,
    )(stay(visibilities), stay(coherencies))

    def gather(value):
        parts = [value] + [exchange(value, "pair", pairs, 2 * m) for m in range(1, zn)]
        own = jnp.stack(parts)
        return own, exchange(own, "pair", pairs, 1)

    own, sib = gather(payload)

    terms = pl.pallas_call(
        lambda *refs: first_kernel(plan, *refs),
        name="first",
        in_specs=[smem, vmem, vmem, vmem, vmem],
        out_specs=vmem,
        out_shape=f32(blocks, k, LANES),
        scratch_shapes=scratch,
        compiler_params=params,
    )(meta, own, sib, vis, coh)

    term_own, term_sib = gather(terms)
    part_own, part_sib, rest = pl.pallas_call(
        lambda *refs: second_kernel(plan, step_size, *refs),
        name="second",
        in_specs=[smem] + [vmem] * 7,
        out_specs=[vmem, vmem, vmem],
        out_shape=[f32(zn, k, LANES), f32(zn, k, LANES), f32(2, k, LANES)],
        scratch_shapes=scratch,
        compiler_params=params,
    )(meta, own, sib, term_own, term_sib, mult_rec, vis, coh)

    crossed = exchange(part_sib, "pair", pairs, 1)
    total = part_own[0] + crossed[0]
    for m in range(1, zn):
        total = total + exchange(part_own[m] + crossed[m], "pair", pairs, 2 * m)
    new_gain = rest[0] + step_size * total
    summed = rest[1] + step_size * total

    others = [exchange(summed, "band", bands, m) for m in range(1, bands)]
    shape = f32(*gains.shape)
    return pl.pallas_call(
        lambda *refs: fit_kernel(plan, fit_matrix(bands, P_SIZE), *refs),
        name="fit",
        in_specs=[vmem] * (2 + len(others)),
        out_specs=[vmem] * 3,
        out_shape=[shape] * 3,
        compiler_params=params,
    )(new_gain, summed, *others)


def solution(mesh):
    placed = (
        P("band", "pair", None, None, None),
        P("band", "pair", None, None, None, None),
        P("pair", None),
        P("pair"),
        P("band", None, None, "pair"),
        P("band", None, None, "pair"),
        P("band", None, None, "pair"),
    )
    return jax.shard_map(
        local,
        mesh=mesh,
        in_specs=placed,
        out_specs=(
            P("band", None, None, "pair"),
            P("band", None, None, "pair"),
            P("band", None, None, "pair"),
        ),
        check_vma=False,
    )
```

profile of v0, /device:TPU:0, one launch (start us, length us, event | category | flops | bytes accessed | tf_op | source)
XLA Modules:
  0.0 52.9 jit_solution(14204804158486029977)
XLA Ops:
  0.6 1.0 %pack.1 = (f32[72,128]{1,0:T(8,128)S(1)}, s32[8,128]{1,0:T(8,128)S(1)}, f32[32,128]{1,0:T(8,128)S(1)}) custom-call(s32[2,2]{1,0:T(2,128)} %refs_0_.2, s32[2]{0:T(128)} %refs_1_.2, f32[1,2,32,64]{3,2,1,0:T(8,128)} %refs_2_.1, f32[1,2,32,64]{3,2,1,0:T(8,128)} %refs_3_.1, f32[1,2,32,64]{3,2,1,0:T(8,128)} %refs_4_.1), custom_call_target="tpu_custom_call" | custom-call | tf_op jit(solution)/shard_map/pack/pallas_call | solution.py:415
  1.6 5.1 %collective-permute-start.2 = (f32[72,128]{1,0:T(8,128)S(1)}, f32[72,128]{1,0:T(8,128)S(1)}, u32[]{:S(2)}, u32[]{:S(2)}) collective-permute-start(f32[72,128]{1,0:T(8,128)S(1)} %get-tuple-element.12), channel_id=1, source_target_pairs={{0,6},{1,7},{2,4},{3,5},{4,2},{5,3},{6,0},{7,1},{8,14},{9,15},{10,... | collective-permute-start | bytes 110600 | tf_op jit(solution)/shard_map/ppermute | solution.py:389
  6.7 0.0 collective-permute-start.1
  6.7 0.6 %collective-permute-start = (f32[72,128]{1,0:T(8,128)S(1)}, f32[72,128]{1,0:T(8,128)S(1)}, u32[]{:S(2)}, u32[]{:S(2)}) collective-permute-start(f32[72,128]{1,0:T(8,128)S(1)} %get-tuple-element.12), channel_id=1, source_target_pairs={{0,2},{1,3},{2,0},{3,1},{4,6},{5,7},{6,4},{7,5},{8,10},{9,11},{10,... | collective-permute-start | bytes 110600 | tf_op jit(solution)/shard_map/ppermute | solution.py:389
  7.4 1.3 %collective-permute-done.2 = f32[72,128]{1,0:T(8,128)S(1)} collective-permute-done((f32[72,128]{1,0:T(8,128)S(1)}, f32[72,128]{1,0:T(8,128)S(1)}, u32[]{:S(2)}, u32[]{:S(2)}) %collective-permute-start.2) | collective-permute-done | bytes 36896 | tf_op jit(solution)/shard_map/ppermute | solution.py:389
  8.7 2.9 %collective-permute-done.1 = f32[72,128]{1,0:T(8,128)S(1)} collective-permute-done((f32[72,128]{1,0:T(8,128)S(1)}, f32[72,128]{1,0:T(8,128)S(1)}, u32[]{:S(2)}, u32[]{:S(2)}) %collective-permute-start.1) | collective-permute-done | bytes 36896 | tf_op jit(solution)/shard_map/ppermute | solution.py:389
  11.6 0.0 collective-permute-done
  11.6 0.1 collective-permute-start.3
  11.7 1.7 %load.1 = (f32[2,2,8,1024]{3,2,1,0:T(8,128)S(1)}, f32[2,8,2,32,1024]{4,3,2,1,0:T(8,128)S(1)}) custom-call(f32[1,2,8,2,1024]{4,3,2,1,0:T(2,128)} %refs_0_.3, bf16[1,2,8,2,32,1024]{5,4,3,2,1,0:T(8,128)(2,1)} %refs_1_.3), custom_call_target="tpu_custom_call" | custom-call | tf_op jit(solution)/shard_map/load/pallas_call | solution.py:430
  13.4 0.0 collective-permute-done.3.refs_2_
  13.4 7.2 %first.1 = f32[2,32,128]{2,1,0:T(8,128)S(1)} custom-call(s32[8,128]{1,0:T(8,128)S(1)} %get-tuple-element.11.refs_0_, f32[4,72,128]{2,1,0:T(8,128)S(1)} %pad_maximum_fusion.refs_1_, f32[4,72,128]{2,1,0:T(8,128)S(1)} %collective-permute-done.3.refs_2_, f32[2,2,8,1024]{3,2,1,0:T(8,128)S(1)} %get-tuple-element.13.refs_3_.refs_6_, ...), custom_call_target="tpu_custom_call" | custom-call | tf_op jit(solution)/shard_map/first/pallas_call | solution.py:451
  20.6 1.5 %collective-permute-start.6 = (f32[2,32,128]{2,1,0:T(8,128)S(1)}, f32[2,32,128]{2,1,0:T(8,128)S(1)}, u32[]{:S(2)}, u32[]{:S(2)}) collective-permute-start(f32[2,32,128]{2,1,0:T(8,128)S(1)} %first.1), channel_id=1, source_target_pairs={{0,6},{1,7},{2,4},{3,5},{4,2},{5,3},{6,0},{7,1},{8,14},{9,15},{10,... | collective-permute-start | bytes 98312 | tf_op jit(solution)/shard_map/ppermute | solution.py:389
  22.1 0.6 %collective-permute-start.5 = (f32[2,32,128]{2,1,0:T(8,128)S(1)}, f32[2,32,128]{2,1,0:T(8,128)S(1)}, u32[]{:S(2)}, u32[]{:S(2)}) collective-permute-start(f32[2,32,128]{2,1,0:T(8,128)S(1)} %first.1), channel_id=1, source_target_pairs={{0,4},{1,5},{2,6},{3,7},{4,0},{5,1},{6,2},{7,3},{8,12},{9,13},{10,... | collective-permute-start | bytes 98312 | tf_op jit(solution)/shard_map/ppermute | solution.py:389
  22.8 2.3 %collective-permute-start.4 = (f32[2,32,128]{2,1,0:T(8,128)S(1)}, f32[2,32,128]{2,1,0:T(8,128)S(1)}, u32[]{:S(2)}, u32[]{:S(2)}) collective-permute-start(f32[2,32,128]{2,1,0:T(8,128)S(1)} %first.1), channel_id=1, source_target_pairs={{0,2},{1,3},{2,0},{3,1},{4,6},{5,7},{6,4},{7,5},{8,10},{9,11},{10,... | collective-permute-start | bytes 98312 | tf_op jit(solution)/shard_map/ppermute | solution.py:389
  25.1 1.4 %collective-permute-done.6 = f32[2,32,128]{2,1,0:T(8,128)S(1)} collective-permute-done((f32[2,32,128]{2,1,0:T(8,128)S(1)}, f32[2,32,128]{2,1,0:T(8,128)S(1)}, u32[]{:S(2)}, u32[]{:S(2)}) %collective-permute-start.6) | collective-permute-done | bytes 32800 | tf_op jit(solution)/shard_map/ppermute | solution.py:389
  26.4 1.0 %collective-permute-done.5 = f32[2,32,128]{2,1,0:T(8,128)S(1)} collective-permute-done((f32[2,32,128]{2,1,0:T(8,128)S(1)}, f32[2,32,128]{2,1,0:T(8,128)S(1)}, u32[]{:S(2)}, u32[]{:S(2)}) %collective-permute-start.5) | collective-permute-done | bytes 32800 | tf_op jit(solution)/shard_map/ppermute | solution.py:389
  27.4 0.2 collective-permute-done.4
  27.7 0.1 collective-permute-start.7
  27.7 1.3 %collective-permute-done.7.refs_4_ = f32[4,2,32,128]{3,2,1,0:T(8,128)S(1)} collective-permute-done((f32[4,2,32,128]{3,2,1,0:T(8,128)S(1)}, f32[4,2,32,128]{3,2,1,0:T(8,128)S(1)}, u32[]{:S(2)}, u32[]{:S(2)}) %collective-permute-start.7) | collective-permute-done | bytes 131104 | tf_op jit(solution)/shard_map/ppermute | solution.py:389
  29.1 7.4 %second.1 = (f32[4,32,128]{2,1,0:T(8,128)S(1)}, f32[4,32,128]{2,1,0:T(8,128)S(1)}, f32[2,32,128]{2,1,0:T(8,128)S(1)}) custom-call(s32[8,128]{1,0:T(8,128)S(1)} %get-tuple-element.11.refs_0_, f32[4,72,128]{2,1,0:T(8,128)S(1)} %pad_maximum_fusion.refs_1_, f32[4,72,128]{2,1,0:T(8,128)S(1)} %collective-permute-done.3.refs_2_, ...), custom_call_target="tpu_custom_call" | custom-call | tf_op jit(solution)/shard_map/second/pallas_call | solution.py:462
  36.5 0.2 collective-permute-start.8
  36.7 1.1 %collective-permute-done.8 = f32[4,32,128]{2,1,0:T(8,128)S(1)} collective-permute-done((f32[4,32,128]{2,1,0:T(8,128)S(1)}, f32[4,32,128]{2,1,0:T(8,128)S(1)}, u32[]{:S(2)}, u32[]{:S(2)}) %collective-permute-start.8) | collective-permute-done | bytes 65568 | tf_op jit(solution)/shard_map/ppermute | solution.py:389
  37.8 1.4 %collective-permute-start.9 = (f32[32,128]{1,0:T(8,128)S(1)}, f32[32,128]{1,0:T(8,128)S(1)}, u32[]{:S(2)}, u32[]{:S(2)}) collective-permute-start(f32[32,128]{1,0:T(8,128)S(1)} %get-tuple-element.21), channel_id=1, source_target_pairs={{0,2},{1,3},{2,0},{3,1},{4,6},{5,7},{6,4},{7,5},{8,10},{9,11},{10,... | collective-permute-start | bytes 49160 | tf_op jit(solution)/shard_map/ppermute | solution.py:389
  39.2 1.5 %collective-permute-start.11 = (f32[32,128]{1,0:T(8,128)S(1)}, f32[32,128]{1,0:T(8,128)S(1)}, u32[]{:S(2)}, u32[]{:S(2)}) collective-permute-start(f32[32,128]{1,0:T(8,128)S(1)} %get-tuple-element.22), channel_id=1, source_target_pairs={{0,6},{1,7},{2,4},{3,5},{4,2},{5,3},{6,0},{7,1},{8,14},{9,15},{10,... | collective-permute-start | bytes 49160 | tf_op jit(solution)/shard_map/ppermute | solution.py:389
  40.7 0.7 %collective-permute-start.10 = (f32[32,128]{1,0:T(8,128)S(1)}, f32[32,128]{1,0:T(8,128)S(1)}, u32[]{:S(2)}, u32[]{:S(2)}) collective-permute-start(f32[32,128]{1,0:T(8,128)S(1)} %get-tuple-element.23), channel_id=1, source_target_pairs={{0,4},{1,5},{2,6},{3,7},{4,0},{5,1},{6,2},{7,3},{8,12},{9,13},{10,... | collective-permute-start | bytes 49160 | tf_op jit(solution)/shard_map/ppermute | solution.py:389
  41.4 0.2 collective-permute-done.9
  41.6 3.1 %collective-permute-done.11 = f32[32,128]{1,0:T(8,128)S(1)} collective-permute-done((f32[32,128]{1,0:T(8,128)S(1)}, f32[32,128]{1,0:T(8,128)S(1)}, u32[]{:S(2)}, u32[]{:S(2)}) %collective-permute-start.11) | collective-permute-done | bytes 16416 | tf_op jit(solution)/shard_map/ppermute | solution.py:389
  44.8 0.7 %collective-permute-done.10 = f32[32,128]{1,0:T(8,128)S(1)} collective-permute-done((f32[32,128]{1,0:T(8,128)S(1)}, f32[32,128]{1,0:T(8,128)S(1)}, u32[]{:S(2)}, u32[]{:S(2)}) %collective-permute-start.10) | collective-permute-done | bytes 16416 | tf_op jit(solution)/shard_map/ppermute | solution.py:389
  45.5 2.5 %collective-permute-start.14 = (f32[32,128]{1,0:T(8,128)S(1)}, f32[32,128]{1,0:T(8,128)S(1)}, u32[]{:S(2)}, u32[]{:S(2)}) collective-permute-start(f32[32,128]{1,0:T(8,128)S(1)} %get-tuple-element.19.refs_1_), channel_id=1, source_target_pairs={{0,24},{8,16},{16,8},{24,0},{1,25},{9,17},{17,9},{25,1},{2,26},{10... | collective-permute-start | bytes 49160 | tf_op jit(solution)/shard_map/ppermute | solution.py:389
  48.0 0.5 collective-permute-start.13
  48.5 0.5 %collective-permute-start.12 = (f32[32,128]{1,0:T(8,128)S(1)}, f32[32,128]{1,0:T(8,128)S(1)}, u32[]{:S(2)}, u32[]{:S(2)}) collective-permute-start(f32[32,128]{1,0:T(8,128)S(1)} %get-tuple-element.19.refs_1_), channel_id=1, source_target_pairs={{0,8},{8,0},{16,24},{24,16},{1,9},{9,1},{17,25},{25,17},{2,10},{10... | collective-permute-start | bytes 49160 | tf_op jit(solution)/shard_map/ppermute | solution.py:389
  49.0 1.2 %collective-permute-done.14.refs_4_ = f32[32,128]{1,0:T(8,128)S(1)} collective-permute-done((f32[32,128]{1,0:T(8,128)S(1)}, f32[32,128]{1,0:T(8,128)S(1)}, u32[]{:S(2)}, u32[]{:S(2)}) %collective-permute-start.14) | collective-permute-done | bytes 16416 | tf_op jit(solution)/shard_map/ppermute | solution.py:389
  50.3 1.4 %collective-permute-done.13.refs_3_ = f32[32,128]{1,0:T(8,128)S(1)} collective-permute-done((f32[32,128]{1,0:T(8,128)S(1)}, f32[32,128]{1,0:T(8,128)S(1)}, u32[]{:S(2)}, u32[]{:S(2)}) %collective-permute-start.13) | collective-permute-done | bytes 16416 | tf_op jit(solution)/shard_map/ppermute | solution.py:389
  51.7 0.5 collective-permute-done.12.refs_2_
  52.2 0.7 %fit.1 = (f32[1,2,32,64]{3,2,1,0:T(8,128)}, f32[1,2,32,64]{3,2,1,0:T(8,128)}, f32[1,2,32,64]{3,2,1,0:T(8,128)}) custom-call(f32[32,128]{1,0:T(8,128)S(1)} %bitcast_add_fusion.1.refs_0_, f32[32,128]{1,0:T(8,128)S(1)} %get-tuple-element.19.refs_1_, f32[32,128]{1,0:T(8,128)S(1)} %collective-permute-done.12.refs_2_, ...), custom_call_target="tpu_custom_call" | custom-call | tf_op jit(solution)/shard_map/fit/pallas_call | solution.py:481
  (5 shorter events, 0.0 us)
Async XLA Ops:
  1.6 7.1 %collective-permute-start.2 = (f32[72,128]{1,0:T(8,128)S(1)}, f32[72,128]{1,0:T(8,128)S(1)}, u32[]{:S(2)}, u32[]{:S(2)}) collective-permute-start(f32[72,128]{1,0:T(8,128)S(1)} %get-tuple-element.12), channel_id=1, source_target_pairs={{0,6},{1,7},{2,4},{3,5},{4,2},{5,3},{6,0},{7,1},{8,14},{9,15},{10,... | collective-permute-start | bytes 110600 | tf_op jit(solution)/shard_map/ppermute | solution.py:389
  6.7 4.9 %collective-permute-start.1 = (f32[72,128]{1,0:T(8,128)S(1)}, f32[72,128]{1,0:T(8,128)S(1)}, u32[]{:S(2)}, u32[]{:S(2)}) collective-permute-start(f32[72,128]{1,0:T(8,128)S(1)} %get-tuple-element.12), channel_id=1, source_target_pairs={{0,4},{1,5},{2,6},{3,7},{4,0},{5,1},{6,2},{7,3},{8,12},{9,13},{10,... | collective-permute-start | bytes 110600 | tf_op jit(solution)/shard_map/ppermute | solution.py:389
  6.7 4.9 %collective-permute-start = (f32[72,128]{1,0:T(8,128)S(1)}, f32[72,128]{1,0:T(8,128)S(1)}, u32[]{:S(2)}, u32[]{:S(2)}) collective-permute-start(f32[72,128]{1,0:T(8,128)S(1)} %get-tuple-element.12), channel_id=1, source_target_pairs={{0,2},{1,3},{2,0},{3,1},{4,6},{5,7},{6,4},{7,5},{8,10},{9,11},{10,... | collective-permute-start | bytes 110600 | tf_op jit(solution)/shard_map/ppermute | solution.py:389
  11.6 1.8 %collective-permute-start.3 = (f32[4,72,128]{2,1,0:T(8,128)S(1)}, f32[4,72,128]{2,1,0:T(8,128)S(1)}, u32[]{:S(2)}, u32[]{:S(2)}) collective-permute-start(f32[4,72,128]{2,1,0:T(8,128)S(1)} %pad_maximum_fusion.refs_1_), channel_id=1, source_target_pairs={{0,1},{1,0},{2,3},{3,2},{4,5},{5,4},{6,7},{7,6},{8,9},{9,8},{10,11... | collective-permute-start | bytes 442376 | tf_op jit(solution)/shard_map/ppermute | solution.py:389
  20.6 5.8 %collective-permute-start.6 = (f32[2,32,128]{2,1,0:T(8,128)S(1)}, f32[2,32,128]{2,1,0:T(8,128)S(1)}, u32[]{:S(2)}, u32[]{:S(2)}) collective-permute-start(f32[2,32,128]{2,1,0:T(8,128)S(1)} %first.1), channel_id=1, source_target_pairs={{0,6},{1,7},{2,4},{3,5},{4,2},{5,3},{6,0},{7,1},{8,14},{9,15},{10,... | collective-permute-start | bytes 98312 | tf_op jit(solution)/shard_map/ppermute | solution.py:389
  22.1 5.3 %collective-permute-start.5 = (f32[2,32,128]{2,1,0:T(8,128)S(1)}, f32[2,32,128]{2,1,0:T(8,128)S(1)}, u32[]{:S(2)}, u32[]{:S(2)}) collective-permute-start(f32[2,32,128]{2,1,0:T(8,128)S(1)} %first.1), channel_id=1, source_target_pairs={{0,4},{1,5},{2,6},{3,7},{4,0},{5,1},{6,2},{7,3},{8,12},{9,13},{10,... | collective-permute-start | bytes 98312 | tf_op jit(solution)/shard_map/ppermute | solution.py:389
  22.8 4.9 %collective-permute-start.4 = (f32[2,32,128]{2,1,0:T(8,128)S(1)}, f32[2,32,128]{2,1,0:T(8,128)S(1)}, u32[]{:S(2)}, u32[]{:S(2)}) collective-permute-start(f32[2,32,128]{2,1,0:T(8,128)S(1)} %first.1), channel_id=1, source_target_pairs={{0,2},{1,3},{2,0},{3,1},{4,6},{5,7},{6,4},{7,5},{8,10},{9,11},{10,... | collective-permute-start | bytes 98312 | tf_op jit(solution)/shard_map/ppermute | solution.py:389
  27.7 1.4 %collective-permute-start.7 = (f32[4,2,32,128]{3,2,1,0:T(8,128)S(1)}, f32[4,2,32,128]{3,2,1,0:T(8,128)S(1)}, u32[]{:S(2)}, u32[]{:S(2)}) collective-permute-start(f32[4,2,32,128]{3,2,1,0:T(8,128)S(1)} %pad_maximum_fusion.1.refs_3_), channel_id=1, source_target_pairs={{0,1},{1,0},{2,3},{3,2},{4,5},{5,4},{6,7},{7,6},{8,9},{9,8},{10,11... | collective-permute-start | bytes 393224 | tf_op jit(solution)/shard_map/ppermute | solution.py:389
  36.5 1.3 %collective-permute-start.8 = (f32[4,32,128]{2,1,0:T(8,128)S(1)}, f32[4,32,128]{2,1,0:T(8,128)S(1)}, u32[]{:S(2)}, u32[]{:S(2)}) collective-permute-start(f32[4,32,128]{2,1,0:T(8,128)S(1)} %get-tuple-element.18), channel_id=1, source_target_pairs={{0,1},{1,0},{2,3},{3,2},{4,5},{5,4},{6,7},{7,6},{8,9},{9,8},{10,11... | collective-permute-start | bytes 196616 | tf_op jit(solution)/shard_map/ppermute | solution.py:389
  37.8 3.8 %collective-permute-start.9 = (f32[32,128]{1,0:T(8,128)S(1)}, f32[32,128]{1,0:T(8,128)S(1)}, u32[]{:S(2)}, u32[]{:S(2)}) collective-permute-start(f32[32,128]{1,0:T(8,128)S(1)} %get-tuple-element.21), channel_id=1, source_target_pairs={{0,2},{1,3},{2,0},{3,1},{4,6},{5,7},{6,4},{7,5},{8,10},{9,11},{10,... | collective-permute-start | bytes 49160 | tf_op jit(solution)/shard_map/ppermute | solution.py:389
  39.2 5.5 %collective-permute-start.11 = (f32[32,128]{1,0:T(8,128)S(1)}, f32[32,128]{1,0:T(8,128)S(1)}, u32[]{:S(2)}, u32[]{:S(2)}) collective-permute-start(f32[32,128]{1,0:T(8,128)S(1)} %get-tuple-element.22), channel_id=1, source_target_pairs={{0,6},{1,7},{2,4},{3,5},{4,2},{5,3},{6,0},{7,1},{8,14},{9,15},{10,... | collective-permute-start | bytes 49160 | tf_op jit(solution)/shard_map/ppermute | solution.py:389
  40.7 4.8 %collective-permute-start.10 = (f32[32,128]{1,0:T(8,128)S(1)}, f32[32,128]{1,0:T(8,128)S(1)}, u32[]{:S(2)}, u32[]{:S(2)}) collective-permute-start(f32[32,128]{1,0:T(8,128)S(1)} %get-tuple-element.23), channel_id=1, source_target_pairs={{0,4},{1,5},{2,6},{3,7},{4,0},{5,1},{6,2},{7,3},{8,12},{9,13},{10,... | collective-permute-start | bytes 49160 | tf_op jit(solution)/shard_map/ppermute | solution.py:389
  45.5 4.8 %collective-permute-start.14 = (f32[32,128]{1,0:T(8,128)S(1)}, f32[32,128]{1,0:T(8,128)S(1)}, u32[]{:S(2)}, u32[]{:S(2)}) collective-permute-start(f32[32,128]{1,0:T(8,128)S(1)} %get-tuple-element.19.refs_1_), channel_id=1, source_target_pairs={{0,24},{8,16},{16,8},{24,0},{1,25},{9,17},{17,9},{25,1},{2,26},{10... | collective-permute-start | bytes 49160 | tf_op jit(solution)/shard_map/ppermute | solution.py:389
  48.0 3.7 %collective-permute-start.13 = (f32[32,128]{1,0:T(8,128)S(1)}, f32[32,128]{1,0:T(8,128)S(1)}, u32[]{:S(2)}, u32[]{:S(2)}) collective-permute-start(f32[32,128]{1,0:T(8,128)S(1)} %get-tuple-element.19.refs_1_), channel_id=1, source_target_pairs={{0,16},{8,24},{16,0},{24,8},{1,17},{9,25},{17,1},{25,9},{2,18},{10... | collective-permute-start | bytes 49160 | tf_op jit(solution)/shard_map/ppermute | solution.py:389
  48.5 3.7 %collective-permute-start.12 = (f32[32,128]{1,0:T(8,128)S(1)}, f32[32,128]{1,0:T(8,128)S(1)}, u32[]{:S(2)}, u32[]{:S(2)}) collective-permute-start(f32[32,128]{1,0:T(8,128)S(1)} %get-tuple-element.19.refs_1_), channel_id=1, source_target_pairs={{0,8},{8,0},{16,24},{24,16},{1,9},{9,1},{17,25},{25,17},{2,10},{10... | collective-permute-start | bytes 49160 | tf_op jit(solution)/shard_map/ppermute | solution.py:389
where the time goes:
time: 53.2 us; the launch traced here: 52.9 us
  Pallas kernels  18 us (34%)
  starting transfers between devices  17.7 us (33%)
  waiting for transfers between devices  16.5 us (31%)
  between operations  0.71 us (1%)
    ppermute x15, starting transfers between devices, exchange(): return lax.ppermute(value, axis, [(i, i ^ mask) for i in range(size)])  17.7 us
    ppermute x15, waiting for transfers between devices, exchange(): return lax.ppermute(value, axis, [(i, i ^ mask) for i in range(size)])  16.5 us
    pallas_call x1, Pallas kernels, local(): pl.pallas_call(lambda *refs: second_kernel(plan, step_size, *refs), name=...  7.43 us
    pallas_call x1, Pallas kernels, local(): pl.pallas_call(lambda *refs: first_kernel(plan, *refs), name='first', in_...  7.21 us
    pallas_call x1, Pallas kernels, local(): pl.pallas_call(lambda *refs: load_kernel(plan, *refs), name='load', in_sp...  1.67 us
  transfers between devices with their start and end apart: 15, of which 13 were waited for; matrix products, arithmetic and copies ran while one was open for 0% of the time, Pallas kernels for 3%

commit v1 on v0

--- a/solution.py
+++ b/solution.py
@@ -112,9 +112,13 @@
 
 def merge(low, first, second, shift, axis):
     size = first.shape[axis]
-    if 2 * shift == size:
+    if axis == 1 or 2 * shift == size:
         mixed = jnp.where(low, second, first)
-        return jnp.where(low, first, second) + pltpu.roll(mixed, shift, axis)
+        if 2 * shift == size:
+            mixed = pltpu.roll(mixed, shift, axis)
+        else:
+            mixed = take(mixed, lax.broadcasted_iota(jnp.int32, mixed.shape, 1) ^ shift)
+        return jnp.where(low, first, second) + mixed
     up = first + pltpu.roll(first, size - shift, axis)
     down = second + pltpu.roll(second, shift, axis)
     return jnp.where(low, up, down)
@@ -199,7 +203,7 @@
             vis_ref[n, part] = vis_buf[n, :, part, :]
 
 
-def block_gradients(plan, meta_ref, tile_gains, vis_ref, coh_ref, right_ref, left_ref, second_ref, first_ref):
+def block_gradients(plan, meta_ref, tile_gains, vis_ref, coh_ref, right_ref, left_ref, wide_ref, second_ref, first_ref):
     k, times, steps = plan.k, plan.times, plan.steps
     lane_k = plan.lane()
     lane = plan.lane(8)
@@ -210,10 +214,12 @@
         right_ref[n, 1] = take(right, TILE + lane_k % TILE)
         second_ref[n] = jnp.zeros((2, k, LANES), jnp.float32)
 
-    def lefts(n, index):
+    def lefts(q):
+        n, index, _ = where_is(q)
         left = left_ref[n]
         spot = index * GROUP + lane_k // TILE
-        return take(left, spot), take(left, TILE + spot)
+        wide_ref[n, index, 0] = take(left, spot)
+        wide_ref[n, index, 1] = take(left, TILE + spot)
 
     def where_is(q):
         n = q // steps
@@ -222,7 +228,7 @@
 
     def residual(q):
         n, index, lanes = where_is(q)
-        lr, li = lefts(n, index)
+        lr, li = wide_ref[n, index, 0], wide_ref[n, index, 1]
         rr, ri = right_ref[n, 0], right_ref[n, 1]
         pr = lr * rr + li * ri
         pi = li * rr - lr * ri
@@ -258,32 +264,35 @@
             im = i * cr - r * ci
             acc_re = re if acc_re is None else acc_re + re
             acc_im = im if acc_im is None else acc_im + im
-        lr, li = lefts(n, index)
+        lr, li = wide_ref[n, index, 0], wide_ref[n, index, 1]
         rr, ri = right_ref[n, 0], right_ref[n, 1]
         second_ref[n, 0] = second_ref[n, 0] + (acc_re * lr + acc_im * li)
         second_ref[n, 1] = second_ref[n, 1] + (acc_re * li - acc_im * lr)
-        parts = eights(acc_re * rr - acc_im * ri) + eights(acc_re * ri + acc_im * rr)
-        (total,) = merge_all(parts, (16, 8, 4), 1)
-        for shift in (2, 1):
-            (total,) = merge_all([total, total], (shift,), 1)
-        first_ref[n, index] = total
+        first_ref[n, index, 0] = acc_re * rr - acc_im * ri
+        first_ref[n, index, 1] = acc_re * ri + acc_im * rr
+
+    final = plan.blocks * steps - 1
 
     def step(q, errors):
+        lefts(jnp.minimum(q + 2, final))
         following = residual(q + 1)
         gradient(q, errors)
         return following
 
-    final = plan.blocks * steps - 1
+    lefts(0)
+    lefts(1)
     gradient(final, lax.fori_loop(0, final, step, residual(0)))
 
     results = []
     for n in range(plan.blocks):
-        packed = []
-        for base in range(0, steps, 4):
-            value = first_ref[n, base]
-            for r in range(1, 4):
-                value = jnp.where(lane % 4 == r, first_ref[n, base + r], value)
-            packed.append(value)
+        items = [
+            first_ref[n, 4 * h + r, part, 8 * group : 8 * group + 8, :]
+            for part in range(2)
+            for group in range(k // 8)
+            for r in range(4)
+            for h in range(steps // 4)
+        ]
+        packed = merge_all(items, (16, 8, 4, 2, 1), 1)
         seconds = merge_all(eights(second_ref[n, 0]) + eights(second_ref[n, 1]), (64, 32), 1)
         part, spot = lane // TILE % 2, lane % TILE
         rows = []
@@ -407,8 +416,9 @@
     scratch = [
         pltpu.VMEM((blocks, 2, k, LANES), jnp.float32),
         pltpu.VMEM((blocks, k, LANES), jnp.float32),
+        pltpu.VMEM((blocks, plan.steps, 2, k, LANES), jnp.float32),
         pltpu.VMEM((blocks, 2, k, LANES), jnp.float32),
-        pltpu.VMEM((blocks, plan.steps, 8, LANES), jnp.float32),
+        pltpu.VMEM((blocks, plan.steps, 2, k, LANES), jnp.float32),
     ]
     params = pltpu.CompilerParams(vmem_limit_bytes=16 << 20)
 

time: 53.2 us -> 45.8 us (0.86)
  Pallas kernels: 18 us -> 10.6 us
    pallas_call x1, Pallas kernels: 7.21 us -> 3.51 us  [local(): pl.pallas_call(lambda *refs: first_kernel(plan, *refs), name='first', in_...]
    pallas_call x1, Pallas kernels: 7.43 us -> 3.74 us  [local(): pl.pallas_call(lambda *refs: second_kernel(plan, step_size, *refs), name=...]
  transfers between devices with their start and end apart: 15 -> 15, of which waited for: 13 -> 13; matrix products, arithmetic and copies ran while one was open for 0% -> 0% of each run, Pallas kernels for 3% -> 4%
where the time goes in v1:
time: 45.8 us; the launch traced here: 45.6 us
  starting transfers between devices  17.7 us (39%)
  waiting for transfers between devices  16.5 us (36%)
  Pallas kernels  10.6 us (23%)
  between operations  0.71 us (2%)
    ppermute x15, starting transfers between devices, exchange(): return lax.ppermute(value, axis, [(i, i ^ mask) for i in range(size)])  17.7 us
    ppermute x15, waiting for transfers between devices, exchange(): return lax.ppermute(value, axis, [(i, i ^ mask) for i in range(size)])  16.5 us
    pallas_call x1, Pallas kernels, local(): pl.pallas_call(lambda *refs: second_kernel(plan, step_size, *refs), name=...  3.74 us
    pallas_call x1, Pallas kernels, local(): pl.pallas_call(lambda *refs: first_kernel(plan, *refs), name='first', in_...  3.51 us
    pallas_call x1, Pallas kernels, local(): pl.pallas_call(lambda *refs: load_kernel(plan, *refs), name='load', in_sp...  1.67 us
    pallas_call x1, Pallas kernels, local(): pl.pallas_call(lambda *refs: pack_kernel(plan, *refs), name='pack', in_sp...  0.96 us
  transfers between devices with their start and end apart: 15, of which 13 were waited for; matrix products, arithmetic and copies ran while one was open for 0% of the time, Pallas kernels for 4%

profile of v1, /device:TPU:0, one launch (start us, length us, event | category | flops | bytes accessed | tf_op | source)
XLA Modules:
  0.0 45.6 jit_solution(2446118562159429592)
XLA Ops:
  0.6 1.0 %pack.1 = (f32[72,128]{1,0:T(8,128)S(1)}, s32[8,128]{1,0:T(8,128)S(1)}, f32[32,128]{1,0:T(8,128)S(1)}) custom-call(s32[2,2]{1,0:T(2,128)} %refs_0_.2, s32[2]{0:T(128)} %refs_1_.2, f32[1,2,32,64]{3,2,1,0:T(8,128)} %refs_2_.1, f32[1,2,32,64]{3,2,1,0:T(8,128)} %refs_3_.1, f32[1,2,32,64]{3,2,1,0:T(8,128)} %refs_4_.1), custom_call_target="tpu_custom_call" | custom-call | tf_op jit(solution)/shard_map/pack/pallas_call | solution.py:425
  1.6 5.1 %collective-permute-start.2 = (f32[72,128]{1,0:T(8,128)S(1)}, f32[72,128]{1,0:T(8,128)S(1)}, u32[]{:S(2)}, u32[]{:S(2)}) collective-permute-start(f32[72,128]{1,0:T(8,128)S(1)} %get-tuple-element.12), channel_id=1, source_target_pairs={{0,6},{1,7},{2,4},{3,5},{4,2},{5,3},{6,0},{7,1},{8,14},{9,15},{10,... | collective-permute-start | bytes 110600 | tf_op jit(solution)/shard_map/ppermute | solution.py:398
  6.7 0.0 collective-permute-start.1
  6.7 0.6 %collective-permute-start = (f32[72,128]{1,0:T(8,128)S(1)}, f32[72,128]{1,0:T(8,128)S(1)}, u32[]{:S(2)}, u32[]{:S(2)}) collective-permute-start(f32[72,128]{1,0:T(8,128)S(1)} %get-tuple-element.12), channel_id=1, source_target_pairs={{0,2},{1,3},{2,0},{3,1},{4,6},{5,7},{6,4},{7,5},{8,10},{9,11},{10,... | collective-permute-start | bytes 110600 | tf_op jit(solution)/shard_map/ppermute | solution.py:398
  7.4 1.3 %collective-permute-done.2 = f32[72,128]{1,0:T(8,128)S(1)} collective-permute-done((f32[72,128]{1,0:T(8,128)S(1)}, f32[72,128]{1,0:T(8,128)S(1)}, u32[]{:S(2)}, u32[]{:S(2)}) %collective-permute-start.2) | collective-permute-done | bytes 36896 | tf_op jit(solution)/shard_map/ppermute | solution.py:398
  8.7 2.9 %collective-permute-done.1 = f32[72,128]{1,0:T(8,128)S(1)} collective-permute-done((f32[72,128]{1,0:T(8,128)S(1)}, f32[72,128]{1,0:T(8,128)S(1)}, u32[]{:S(2)}, u32[]{:S(2)}) %collective-permute-start.1) | collective-permute-done | bytes 36896 | tf_op jit(solution)/shard_map/ppermute | solution.py:398
  11.6 0.0 collective-permute-done
  11.6 0.1 collective-permute-start.3
  11.7 1.7 %load.1 = (f32[2,2,8,1024]{3,2,1,0:T(8,128)S(1)}, f32[2,8,2,32,1024]{4,3,2,1,0:T(8,128)S(1)}) custom-call(f32[1,2,8,2,1024]{4,3,2,1,0:T(2,128)} %refs_0_.3, bf16[1,2,8,2,32,1024]{5,4,3,2,1,0:T(8,128)(2,1)} %refs_1_.3), custom_call_target="tpu_custom_call" | custom-call | tf_op jit(solution)/shard_map/load/pallas_call | solution.py:440
  13.4 0.0 collective-permute-done.3.refs_2_
  13.4 3.5 %first.1 = f32[2,32,128]{2,1,0:T(8,128)S(1)} custom-call(s32[8,128]{1,0:T(8,128)S(1)} %get-tuple-element.11.refs_0_, f32[4,72,128]{2,1,0:T(8,128)S(1)} %pad_maximum_fusion.refs_1_, f32[4,72,128]{2,1,0:T(8,128)S(1)} %collective-permute-done.3.refs_2_, f32[2,2,8,1024]{3,2,1,0:T(8,128)S(1)} %get-tuple-element.13.refs_3_.refs_6_, ...), custom_call_target="tpu_custom_call" | custom-call | tf_op jit(solution)/shard_map/first/pallas_call | solution.py:461
  16.9 1.5 %collective-permute-start.6 = (f32[2,32,128]{2,1,0:T(8,128)S(1)}, f32[2,32,128]{2,1,0:T(8,128)S(1)}, u32[]{:S(2)}, u32[]{:S(2)}) collective-permute-start(f32[2,32,128]{2,1,0:T(8,128)S(1)} %first.1), channel_id=1, source_target_pairs={{0,6},{1,7},{2,4},{3,5},{4,2},{5,3},{6,0},{7,1},{8,14},{9,15},{10,... | collective-permute-start | bytes 98312 | tf_op jit(solution)/shard_map/ppermute | solution.py:398
  18.4 0.6 %collective-permute-start.5 = (f32[2,32,128]{2,1,0:T(8,128)S(1)}, f32[2,32,128]{2,1,0:T(8,128)S(1)}, u32[]{:S(2)}, u32[]{:S(2)}) collective-permute-start(f32[2,32,128]{2,1,0:T(8,128)S(1)} %first.1), channel_id=1, source_target_pairs={{0,4},{1,5},{2,6},{3,7},{4,0},{5,1},{6,2},{7,3},{8,12},{9,13},{10,... | collective-permute-start | bytes 98312 | tf_op jit(solution)/shard_map/ppermute | solution.py:398
  19.1 2.3 %collective-permute-start.4 = (f32[2,32,128]{2,1,0:T(8,128)S(1)}, f32[2,32,128]{2,1,0:T(8,128)S(1)}, u32[]{:S(2)}, u32[]{:S(2)}) collective-permute-start(f32[2,32,128]{2,1,0:T(8,128)S(1)} %first.1), channel_id=1, source_target_pairs={{0,2},{1,3},{2,0},{3,1},{4,6},{5,7},{6,4},{7,5},{8,10},{9,11},{10,... | collective-permute-start | bytes 98312 | tf_op jit(solution)/shard_map/ppermute | solution.py:398
  21.4 1.4 %collective-permute-done.6 = f32[2,32,128]{2,1,0:T(8,128)S(1)} collective-permute-done((f32[2,32,128]{2,1,0:T(8,128)S(1)}, f32[2,32,128]{2,1,0:T(8,128)S(1)}, u32[]{:S(2)}, u32[]{:S(2)}) %collective-permute-start.6) | collective-permute-done | bytes 32800 | tf_op jit(solution)/shard_map/ppermute | solution.py:398
  22.7 1.0 %collective-permute-done.5 = f32[2,32,128]{2,1,0:T(8,128)S(1)} collective-permute-done((f32[2,32,128]{2,1,0:T(8,128)S(1)}, f32[2,32,128]{2,1,0:T(8,128)S(1)}, u32[]{:S(2)}, u32[]{:S(2)}) %collective-permute-start.5) | collective-permute-done | bytes 32800 | tf_op jit(solution)/shard_map/ppermute | solution.py:398
  23.8 0.2 collective-permute-done.4
  24.0 0.1 collective-permute-start.7
  24.1 1.3 %collective-permute-done.7.refs_4_ = f32[4,2,32,128]{3,2,1,0:T(8,128)S(1)} collective-permute-done((f32[4,2,32,128]{3,2,1,0:T(8,128)S(1)}, f32[4,2,32,128]{3,2,1,0:T(8,128)S(1)}, u32[]{:S(2)}, u32[]{:S(2)}) %collective-permute-start.7) | collective-permute-done | bytes 131104 | tf_op jit(solution)/shard_map/ppermute | solution.py:398
  25.4 3.7 %second.1 = (f32[4,32,128]{2,1,0:T(8,128)S(1)}, f32[4,32,128]{2,1,0:T(8,128)S(1)}, f32[2,32,128]{2,1,0:T(8,128)S(1)}) custom-call(s32[8,128]{1,0:T(8,128)S(1)} %get-tuple-element.11.refs_0_, f32[4,72,128]{2,1,0:T(8,128)S(1)} %pad_maximum_fusion.refs_1_, f32[4,72,128]{2,1,0:T(8,128)S(1)} %collective-permute-done.3.refs_2_, ...), custom_call_target="tpu_custom_call" | custom-call | tf_op jit(solution)/shard_map/second/pallas_call | solution.py:472
  29.1 0.2 collective-permute-start.8
  29.3 1.1 %collective-permute-done.8 = f32[4,32,128]{2,1,0:T(8,128)S(1)} collective-permute-done((f32[4,32,128]{2,1,0:T(8,128)S(1)}, f32[4,32,128]{2,1,0:T(8,128)S(1)}, u32[]{:S(2)}, u32[]{:S(2)}) %collective-permute-start.8) | collective-permute-done | bytes 65568 | tf_op jit(solution)/shard_map/ppermute | solution.py:398
  30.5 1.4 %collective-permute-start.9 = (f32[32,128]{1,0:T(8,128)S(1)}, f32[32,128]{1,0:T(8,128)S(1)}, u32[]{:S(2)}, u32[]{:S(2)}) collective-permute-start(f32[32,128]{1,0:T(8,128)S(1)} %get-tuple-element.21), channel_id=1, source_target_pairs={{0,2},{1,3},{2,0},{3,1},{4,6},{5,7},{6,4},{7,5},{8,10},{9,11},{10,... | collective-permute-start | bytes 49160 | tf_op jit(solution)/shard_map/ppermute | solution.py:398
  31.8 1.5 %collective-permute-start.11 = (f32[32,128]{1,0:T(8,128)S(1)}, f32[32,128]{1,0:T(8,128)S(1)}, u32[]{:S(2)}, u32[]{:S(2)}) collective-permute-start(f32[32,128]{1,0:T(8,128)S(1)} %get-tuple-element.22), channel_id=1, source_target_pairs={{0,6},{1,7},{2,4},{3,5},{4,2},{5,3},{6,0},{7,1},{8,14},{9,15},{10,... | collective-permute-start | bytes 49160 | tf_op jit(solution)/shard_map/ppermute | solution.py:398
  33.3 0.7 %collective-permute-start.10 = (f32[32,128]{1,0:T(8,128)S(1)}, f32[32,128]{1,0:T(8,128)S(1)}, u32[]{:S(2)}, u32[]{:S(2)}) collective-permute-start(f32[32,128]{1,0:T(8,128)S(1)} %get-tuple-element.23), channel_id=1, source_target_pairs={{0,4},{1,5},{2,6},{3,7},{4,0},{5,1},{6,2},{7,3},{8,12},{9,13},{10,... | collective-permute-start | bytes 49160 | tf_op jit(solution)/shard_map/ppermute | solution.py:398
  34.0 0.2 collective-permute-done.9
  34.3 3.1 %collective-permute-done.11 = f32[32,128]{1,0:T(8,128)S(1)} collective-permute-done((f32[32,128]{1,0:T(8,128)S(1)}, f32[32,128]{1,0:T(8,128)S(1)}, u32[]{:S(2)}, u32[]{:S(2)}) %collective-permute-start.11) | collective-permute-done | bytes 16416 | tf_op jit(solution)/shard_map/ppermute | solution.py:398
  37.4 0.7 %collective-permute-done.10 = f32[32,128]{1,0:T(8,128)S(1)} collective-permute-done((f32[32,128]{1,0:T(8,128)S(1)}, f32[32,128]{1,0:T(8,128)S(1)}, u32[]{:S(2)}, u32[]{:S(2)}) %collective-permute-start.10) | collective-permute-done | bytes 16416 | tf_op jit(solution)/shard_map/ppermute | solution.py:398
  38.1 2.5 %collective-permute-start.14 = (f32[32,128]{1,0:T(8,128)S(1)}, f32[32,128]{1,0:T(8,128)S(1)}, u32[]{:S(2)}, u32[]{:S(2)}) collective-permute-start(f32[32,128]{1,0:T(8,128)S(1)} %get-tuple-element.19.refs_1_), channel_id=1, source_target_pairs={{0,24},{8,16},{16,8},{24,0},{1,25},{9,17},{17,9},{25,1},{2,26},{10... | collective-permute-start | bytes 49160 | tf_op jit(solution)/shard_map/ppermute | solution.py:398
  40.6 0.5 %collective-permute-start.13 = (f32[32,128]{1,0:T(8,128)S(1)}, f32[32,128]{1,0:T(8,128)S(1)}, u32[]{:S(2)}, u32[]{:S(2)}) collective-permute-start(f32[32,128]{1,0:T(8,128)S(1)} %get-tuple-element.19.refs_1_), channel_id=1, source_target_pairs={{0,16},{8,24},{16,0},{24,8},{1,17},{9,25},{17,1},{25,9},{2,18},{10... | collective-permute-start | bytes 49160 | tf_op jit(solution)/shard_map/ppermute | solution.py:398
  41.1 0.5 %collective-permute-start.12 = (f32[32,128]{1,0:T(8,128)S(1)}, f32[32,128]{1,0:T(8,128)S(1)}, u32[]{:S(2)}, u32[]{:S(2)}) collective-permute-start(f32[32,128]{1,0:T(8,128)S(1)} %get-tuple-element.19.refs_1_), channel_id=1, source_target_pairs={{0,8},{8,0},{16,24},{24,16},{1,9},{9,1},{17,25},{25,17},{2,10},{10... | collective-permute-start | bytes 49160 | tf_op jit(solution)/shard_map/ppermute | solution.py:398
  41.7 1.2 %collective-permute-done.14.refs_4_ = f32[32,128]{1,0:T(8,128)S(1)} collective-permute-done((f32[32,128]{1,0:T(8,128)S(1)}, f32[32,128]{1,0:T(8,128)S(1)}, u32[]{:S(2)}, u32[]{:S(2)}) %collective-permute-start.14) | collective-permute-done | bytes 16416 | tf_op jit(solution)/shard_map/ppermute | solution.py:398
  42.9 1.4 %collective-permute-done.13.refs_3_ = f32[32,128]{1,0:T(8,128)S(1)} collective-permute-done((f32[32,128]{1,0:T(8,128)S(1)}, f32[32,128]{1,0:T(8,128)S(1)}, u32[]{:S(2)}, u32[]{:S(2)}) %collective-permute-start.13) | collective-permute-done | bytes 16416 | tf_op jit(solution)/shard_map/ppermute | solution.py:398
  44.3 0.5 %collective-permute-done.12.refs_2_ = f32[32,128]{1,0:T(8,128)S(1)} collective-permute-done((f32[32,128]{1,0:T(8,128)S(1)}, f32[32,128]{1,0:T(8,128)S(1)}, u32[]{:S(2)}, u32[]{:S(2)}) %collective-permute-start.12) | collective-permute-done | bytes 16416 | tf_op jit(solution)/shard_map/ppermute | solution.py:398
  44.9 0.7 %fit.1 = (f32[1,2,32,64]{3,2,1,0:T(8,128)}, f32[1,2,32,64]{3,2,1,0:T(8,128)}, f32[1,2,32,64]{3,2,1,0:T(8,128)}) custom-call(f32[32,128]{1,0:T(8,128)S(1)} %bitcast_add_fusion.1.refs_0_, f32[32,128]{1,0:T(8,128)S(1)} %get-tuple-element.19.refs_1_, f32[32,128]{1,0:T(8,128)S(1)} %collective-permute-done.12.refs_2_, ...), custom_call_target="tpu_custom_call" | custom-call | tf_op jit(solution)/shard_map/fit/pallas_call | solution.py:491
  (5 shorter events, 0.0 us)
Async XLA Ops:
  1.6 7.1 %collective-permute-start.2 = (f32[72,128]{1,0:T(8,128)S(1)}, f32[72,128]{1,0:T(8,128)S(1)}, u32[]{:S(2)}, u32[]{:S(2)}) collective-permute-start(f32[72,128]{1,0:T(8,128)S(1)} %get-tuple-element.12), channel_id=1, source_target_pairs={{0,6},{1,7},{2,4},{3,5},{4,2},{5,3},{6,0},{7,1},{8,14},{9,15},{10,... | collective-permute-start | bytes 110600 | tf_op jit(solution)/shard_map/ppermute | solution.py:398
  6.7 4.9 %collective-permute-start.1 = (f32[72,128]{1,0:T(8,128)S(1)}, f32[72,128]{1,0:T(8,128)S(1)}, u32[]{:S(2)}, u32[]{:S(2)}) collective-permute-start(f32[72,128]{1,0:T(8,128)S(1)} %get-tuple-element.12), channel_id=1, source_target_pairs={{0,4},{1,5},{2,6},{3,7},{4,0},{5,1},{6,2},{7,3},{8,12},{9,13},{10,... | collective-permute-start | bytes 110600 | tf_op jit(solution)/shard_map/ppermute | solution.py:398
  6.7 4.9 %collective-permute-start = (f32[72,128]{1,0:T(8,128)S(1)}, f32[72,128]{1,0:T(8,128)S(1)}, u32[]{:S(2)}, u32[]{:S(2)}) collective-permute-start(f32[72,128]{1,0:T(8,128)S(1)} %get-tuple-element.12), channel_id=1, source_target_pairs={{0,2},{1,3},{2,0},{3,1},{4,6},{5,7},{6,4},{7,5},{8,10},{9,11},{10,... | collective-permute-start | bytes 110600 | tf_op jit(solution)/shard_map/ppermute | solution.py:398
  11.6 1.8 %collective-permute-start.3 = (f32[4,72,128]{2,1,0:T(8,128)S(1)}, f32[4,72,128]{2,1,0:T(8,128)S(1)}, u32[]{:S(2)}, u32[]{:S(2)}) collective-permute-start(f32[4,72,128]{2,1,0:T(8,128)S(1)} %pad_maximum_fusion.refs_1_), channel_id=1, source_target_pairs={{0,1},{1,0},{2,3},{3,2},{4,5},{5,4},{6,7},{7,6},{8,9},{9,8},{10,11... | collective-permute-start | bytes 442376 | tf_op jit(solution)/shard_map/ppermute | solution.py:398
  16.9 5.8 %collective-permute-start.6 = (f32[2,32,128]{2,1,0:T(8,128)S(1)}, f32[2,32,128]{2,1,0:T(8,128)S(1)}, u32[]{:S(2)}, u32[]{:S(2)}) collective-permute-start(f32[2,32,128]{2,1,0:T(8,128)S(1)} %first.1), channel_id=1, source_target_pairs={{0,6},{1,7},{2,4},{3,5},{4,2},{5,3},{6,0},{7,1},{8,14},{9,15},{10,... | collective-permute-start | bytes 98312 | tf_op jit(solution)/shard_map/ppermute | solution.py:398
  18.4 5.3 %collective-permute-start.5 = (f32[2,32,128]{2,1,0:T(8,128)S(1)}, f32[2,32,128]{2,1,0:T(8,128)S(1)}, u32[]{:S(2)}, u32[]{:S(2)}) collective-permute-start(f32[2,32,128]{2,1,0:T(8,128)S(1)} %first.1), channel_id=1, source_target_pairs={{0,4},{1,5},{2,6},{3,7},{4,0},{5,1},{6,2},{7,3},{8,12},{9,13},{10,... | collective-permute-start | bytes 98312 | tf_op jit(solution)/shard_map/ppermute | solution.py:398
  19.1 4.9 %collective-permute-start.4 = (f32[2,32,128]{2,1,0:T(8,128)S(1)}, f32[2,32,128]{2,1,0:T(8,128)S(1)}, u32[]{:S(2)}, u32[]{:S(2)}) collective-permute-start(f32[2,32,128]{2,1,0:T(8,128)S(1)} %first.1), channel_id=1, source_target_pairs={{0,2},{1,3},{2,0},{3,1},{4,6},{5,7},{6,4},{7,5},{8,10},{9,11},{10,... | collective-permute-start | bytes 98312 | tf_op jit(solution)/shard_map/ppermute | solution.py:398
  24.0 1.4 %collective-permute-start.7 = (f32[4,2,32,128]{3,2,1,0:T(8,128)S(1)}, f32[4,2,32,128]{3,2,1,0:T(8,128)S(1)}, u32[]{:S(2)}, u32[]{:S(2)}) collective-permute-start(f32[4,2,32,128]{3,2,1,0:T(8,128)S(1)} %pad_maximum_fusion.1.refs_3_), channel_id=1, source_target_pairs={{0,1},{1,0},{2,3},{3,2},{4,5},{5,4},{6,7},{7,6},{8,9},{9,8},{10,11... | collective-permute-start | bytes 393224 | tf_op jit(solution)/shard_map/ppermute | solution.py:398
  29.1 1.3 %collective-permute-start.8 = (f32[4,32,128]{2,1,0:T(8,128)S(1)}, f32[4,32,128]{2,1,0:T(8,128)S(1)}, u32[]{:S(2)}, u32[]{:S(2)}) collective-permute-start(f32[4,32,128]{2,1,0:T(8,128)S(1)} %get-tuple-element.18), channel_id=1, source_target_pairs={{0,1},{1,0},{2,3},{3,2},{4,5},{5,4},{6,7},{7,6},{8,9},{9,8},{10,11... | collective-permute-start | bytes 196616 | tf_op jit(solution)/shard_map/ppermute | solution.py:398
  30.5 3.8 %collective-permute-start.9 = (f32[32,128]{1,0:T(8,128)S(1)}, f32[32,128]{1,0:T(8,128)S(1)}, u32[]{:S(2)}, u32[]{:S(2)}) collective-permute-start(f32[32,128]{1,0:T(8,128)S(1)} %get-tuple-element.21), channel_id=1, source_target_pairs={{0,2},{1,3},{2,0},{3,1},{4,6},{5,7},{6,4},{7,5},{8,10},{9,11},{10,... | collective-permute-start | bytes 49160 | tf_op jit(solution)/shard_map/ppermute | solution.py:398
  31.8 5.5 %collective-permute-start.11 = (f32[32,128]{1,0:T(8,128)S(1)}, f32[32,128]{1,0:T(8,128)S(1)}, u32[]{:S(2)}, u32[]{:S(2)}) collective-permute-start(f32[32,128]{1,0:T(8,128)S(1)} %get-tuple-element.22), channel_id=1, source_target_pairs={{0,6},{1,7},{2,4},{3,5},{4,2},{5,3},{6,0},{7,1},{8,14},{9,15},{10,... | collective-permute-start | bytes 49160 | tf_op jit(solution)/shard_map/ppermute | solution.py:398
  33.3 4.8 %collective-permute-start.10 = (f32[32,128]{1,0:T(8,128)S(1)}, f32[32,128]{1,0:T(8,128)S(1)}, u32[]{:S(2)}, u32[]{:S(2)}) collective-permute-start(f32[32,128]{1,0:T(8,128)S(1)} %get-tuple-element.23), channel_id=1, source_target_pairs={{0,4},{1,5},{2,6},{3,7},{4,0},{5,1},{6,2},{7,3},{8,12},{9,13},{10,... | collective-permute-start | bytes 49160 | tf_op jit(solution)/shard_map/ppermute | solution.py:398
  38.1 4.8 %collective-permute-start.14 = (f32[32,128]{1,0:T(8,128)S(1)}, f32[32,128]{1,0:T(8,128)S(1)}, u32[]{:S(2)}, u32[]{:S(2)}) collective-permute-start(f32[32,128]{1,0:T(8,128)S(1)} %get-tuple-element.19.refs_1_), channel_id=1, source_target_pairs={{0,24},{8,16},{16,8},{24,0},{1,25},{9,17},{17,9},{25,1},{2,26},{10... | collective-permute-start | bytes 49160 | tf_op jit(solution)/shard_map/ppermute | solution.py:398
  40.6 3.7 %collective-permute-start.13 = (f32[32,128]{1,0:T(8,128)S(1)}, f32[32,128]{1,0:T(8,128)S(1)}, u32[]{:S(2)}, u32[]{:S(2)}) collective-permute-start(f32[32,128]{1,0:T(8,128)S(1)} %get-tuple-element.19.refs_1_), channel_id=1, source_target_pairs={{0,16},{8,24},{16,0},{24,8},{1,17},{9,25},{17,1},{25,9},{2,18},{10... | collective-permute-start | bytes 49160 | tf_op jit(solution)/shard_map/ppermute | solution.py:398
  41.1 3.7 %collective-permute-start.12 = (f32[32,128]{1,0:T(8,128)S(1)}, f32[32,128]{1,0:T(8,128)S(1)}, u32[]{:S(2)}, u32[]{:S(2)}) collective-permute-start(f32[32,128]{1,0:T(8,128)S(1)} %get-tuple-element.19.refs_1_), channel_id=1, source_target_pairs={{0,8},{8,0},{16,24},{24,16},{1,9},{9,1},{17,25},{25,17},{2,10},{10... | collective-permute-start | bytes 49160 | tf_op jit(solution)/shard_map/ppermute | solution.py:398

commit v2 on v0

--- a/solution.py
+++ b/solution.py
@@ -12,7 +12,9 @@
 P_SIZE = 8
 TILE = 32
 LANES = 128
+HALF = LANES // 2
 GROUP = LANES // TILE
+PIECES = 2
 
 ridge = 0.05
 penalty = 0.25
@@ -42,8 +44,8 @@
         self.zn = pairs // 2
         self.blocks = blocks
         self.times = times
-        self.cells = cells
         self.steps = cells // LANES
+        self.total = blocks * self.steps
         self.per = stations // TILE
         self.parts = 1 if self.per else TILE // stations
         self.rows = 2 * directions + 8 * ((blocks + 7) // 8)
@@ -63,7 +65,12 @@
 
     def fetch(self, me, own_ref, sib_ref, tile, row):
         lane = self.lane()
-        part, spot = lane // TILE % 2, lane % TILE
+        part, spot = lane // HALF, lane % TILE
+        if self.sl == HALF:
+            device = lax.shift_right_logical(tile, 1)
+            sub = lax.bitwise_and(tile, 1)
+            rec = self.record(me, own_ref, sib_ref, device, row)
+            return jnp.where(sub == 1, pltpu.roll(rec, LANES - TILE, 1), rec)
         if self.per:
             device = tile // self.per
             sub = tile - device * self.per
@@ -76,25 +83,29 @@
             value = here if value is None else jnp.where(spot // self.sl == r, here, value)
         return value
 
-    def place(self, terms, shift, sub):
+    def place(self, terms, side, sub):
         lane = self.lane()
+        if self.sl == HALF:
+            moved = pltpu.roll(terms, TILE if side == 0 else LANES - TILE, 1)
+            return jnp.where(lane // TILE % 2 == sub, jnp.where(sub == side, terms, moved), 0.0)
         part, spot = lane // self.sl % 2, lane % self.sl
+        start = part * HALF + side * TILE
         if self.per:
-            value = take(terms, shift + part * TILE + spot % TILE)
+            value = take(terms, start + spot % TILE)
             keep = spot // TILE == sub
         else:
-            value = take(terms, shift + part * TILE + sub * self.sl + spot)
+            value = take(terms, start + sub * self.sl + spot)
             keep = lane < 2 * self.sl
         return jnp.where(keep, value, 0.0)
 
-    def spread(self, me, tile, terms, shift, own_ref, sib_ref):
+    def spread(self, me, tile, terms, side, own_ref, sib_ref):
         if self.per:
             device = tile // self.per
             spots = [(device, tile - device * self.per)]
         else:
             spots = [(tile * self.parts + r, r) for r in range(self.parts)]
         for device, sub in spots:
-            value = self.place(terms, shift, sub)
+            value = self.place(terms, side, sub)
             same, slot = self.owner(me, device)
             own_ref[slot] = own_ref[slot] + jnp.where(same, value, 0.0)
             sib_ref[slot] = sib_ref[slot] + jnp.where(same, 0.0, value)
@@ -110,23 +121,16 @@
     return jnp.take_along_axis(value, lanes, axis=1, mode="promise_in_bounds")
 
 
-def merge(low, first, second, shift, axis):
-    size = first.shape[axis]
-    if 2 * shift == size:
-        mixed = jnp.where(low, second, first)
-        return jnp.where(low, first, second) + pltpu.roll(mixed, shift, axis)
-    up = first + pltpu.roll(first, size - shift, axis)
-    down = second + pltpu.roll(second, shift, axis)
-    return jnp.where(low, up, down)
-
-
-def merge_all(items, shifts, axis):
-    index = lax.broadcasted_iota(jnp.int32, items[0].shape, axis)
-    for shift in shifts:
-        half = len(items) // 2
-        low = (index & shift) == 0
-        items = [merge(low, items[i], items[i + half], shift, axis) for i in range(half)]
-    return items
+def pieces(value, count):
+    result = []
+    for _ in range(count):
+        result.append(value.astype(jnp.bfloat16))
+        value = value - result[-1].astype(jnp.float32)
+    return result
+
+
+def matmul(lhs, rhs):
+    return jnp.dot(lhs, rhs, preferred_element_type=jnp.float32)
 
 
 def eights(value):
@@ -157,7 +161,7 @@
     for base in range(0, plan.blocks, 8):
         rows = jnp.zeros((8, LANES), jnp.int32)
         for n in range(base, min(base + 8, plan.blocks)):
-            ids = jnp.where(lane < 2 * TILE, tiles_ref[n, 0], tiles_ref[n, 1])
+            ids = jnp.where(lane // TILE % 2 == 0, tiles_ref[n, 0], tiles_ref[n, 1])
             rows = jnp.where(sub == n - base, ids, rows)
             for j, number in enumerate((tiles_ref[n, 0], tiles_ref[n, 1], counts_ref[n])):
                 meta = jnp.where(lane == 3 * n + j, number, meta)
@@ -166,152 +170,175 @@
 
 
 def load_kernel(plan, vis_hbm, coh_hbm, vis_ref, coh_ref, vis_buf, coh_buf, sems):
-    halves = 2
-    cells = plan.cells // halves
+    chunks = 4
+    per = plan.steps // chunks
     copies = []
     for n in range(plan.blocks):
-        for h in range(halves):
-            lanes = pl.ds(h * cells, cells)
+        for c in range(chunks):
+            lanes = pl.ds(c * per * LANES, per * LANES)
             copies.append(
                 pltpu.make_async_copy(
                     coh_hbm.at[0, n, :, :, :, lanes],
                     coh_buf.at[n, :, :, :, lanes],
-                    sems.at[n * halves + h],
+                    sems.at[n * chunks + c],
                 )
             )
-    last = pltpu.make_async_copy(vis_hbm.at[0], vis_buf, sems.at[plan.blocks * halves])
+    last = pltpu.make_async_copy(vis_hbm.at[0], vis_buf, sems.at[plan.blocks * chunks])
     for copy in copies:
         copy.start()
     last.start()
     for n in range(plan.blocks):
-        for h in range(halves):
-            copies[n * halves + h].wait()
-
-            def convert(t, carry, n=n, h=h):
-                lanes = pl.ds(h * cells, cells)
-                coh_ref[n, t, :, :, lanes] = coh_buf[n, t, :, :, lanes].astype(jnp.float32)
+        for c in range(chunks):
+            copies[n * chunks + c].wait()
+
+            def convert(t, carry, n=n, c=c):
+                for index in range(c * per, (c + 1) * per):
+                    lanes = pl.ds(index * LANES, LANES)
+                    real = coh_buf[n, t, 0, :, lanes].astype(jnp.float32)
+                    imag = coh_buf[n, t, 1, :, lanes].astype(jnp.float32)
+                    q = n * plan.steps + index
+                    coh_ref[q, t, 0] = real
+                    coh_ref[q, t, 1] = real + imag
+                    coh_ref[q, t, 2] = real - imag
                 return carry
 
             lax.fori_loop(0, plan.times, convert, 0)
     last.wait()
     for n in range(plan.blocks):
         for part in range(2):
-            vis_ref[n, part] = vis_buf[n, :, part, :]
-
-
-def block_gradients(plan, meta_ref, tile_gains, vis_ref, coh_ref, right_ref, left_ref, second_ref, first_ref):
+            value = vis_buf[n, :, part, :]
+            for index in range(plan.steps):
+                vis_ref[n * plan.steps + index, part] = value[:, index * LANES : (index + 1) * LANES]
+
+
+def table_kernel(plan, spread_ref, narrow_ref, fold_ref):
+    record = lax.broadcasted_iota(jnp.int32, (LANES, LANES), 0)
+    cell = lax.broadcasted_iota(jnp.int32, (LANES, LANES), 1)
+    spread = cell // TILE - record
+    narrow = record // TILE - cell
+    fold = TILE + record % TILE - cell
+    for part in range(2):
+        for index in range(plan.steps):
+            span = slice((2 * index + part) * LANES, (2 * index + part + 1) * LANES)
+            offset = -(part * HALF + index * GROUP)
+            spread_ref[:, span] = jnp.where(spread == offset, 1.0, 0.0).astype(jnp.bfloat16)
+            narrow_ref[span, :] = jnp.where(narrow == offset, 1.0, 0.0).astype(jnp.bfloat16)
+        hit = jnp.where(fold == -part * HALF, 1.0, 0.0).astype(jnp.bfloat16)
+        fold_ref[part * LANES : (part + 1) * LANES, :] = hit
+
+
+def block_gradients(
+    plan, meta_ref, tile_gains, vis_ref, coh_ref, spread_ref, narrow_ref, fold_ref,
+    right_ref, wide_ref, second_ref, first_ref, model_ref, error_ref,
+):
     k, times, steps = plan.k, plan.times, plan.steps
+    shift = steps.bit_length() - 1
     lane_k = plan.lane()
     lane = plan.lane(8)
     sample = lax.broadcasted_iota(jnp.int32, (8, LANES), 0)
+    lefts = [piece for left, _ in tile_gains for piece in pieces(left, 3)]
+    lefts = matmul(jnp.concatenate(lefts, axis=0), spread_ref[...])
+    for n in range(plan.blocks):
+        rows = [lefts[(3 * n + i) * k : (3 * n + i + 1) * k] for i in range(3)]
+        value = rows[0] + rows[1] + rows[2]
+        for index in range(steps):
+            for part in range(2):
+                start = (2 * index + part) * LANES
+                wide_ref[n * steps + index, part] = value[:, start : start + LANES]
     for n, (left, right) in enumerate(tile_gains):
-        left_ref[n] = left
-        right_ref[n, 0] = take(right, lane_k % TILE)
-        right_ref[n, 1] = take(right, TILE + lane_k % TILE)
+        pairs = jnp.where(lane_k // TILE % 2 == 0, right, pltpu.roll(right, TILE, 1))
+        other = pltpu.roll(pairs, HALF, 1)
+        right_ref[n, 0] = jnp.where(lane_k < HALF, pairs, other)
+        right_ref[n, 1] = jnp.where(lane_k < HALF, other, pairs)
         second_ref[n] = jnp.zeros((2, k, LANES), jnp.float32)
 
-    def lefts(n, index):
-        left = left_ref[n]
-        spot = index * GROUP + lane_k // TILE
-        return take(left, spot), take(left, TILE + spot)
-
     def where_is(q):
-        n = q // steps
-        index = q - n * steps
-        return n, index, pl.ds(pl.multiple_of(index * LANES, LANES), LANES)
+        q = jnp.int32(q)
+        return lax.shift_right_logical(q, shift), lax.bitwise_and(q, steps - 1)
 
     def residual(q):
-        n, index, lanes = where_is(q)
-        lr, li = lefts(n, index)
+        n, index = where_is(q)
+        lr, li = wide_ref[q, 0], wide_ref[q, 1]
         rr, ri = right_ref[n, 0], right_ref[n, 1]
         pr = lr * rr + li * ri
         pi = li * rr - lr * ri
-        reals, imags = [], []
+        ps = pr + pi
         for t in range(times):
-            cr = coh_ref[n, t, 0, :, lanes]
-            ci = coh_ref[n, t, 1, :, lanes]
-            reals.append(sum(eights(pr * cr - pi * ci)))
-            imags.append(sum(eights(pr * ci + pi * cr)))
-        none = jnp.zeros((8, LANES), jnp.float32)
-        reals += [none] * (8 - times)
-        imags += [none] * (8 - times)
-        (mr,) = merge_all(reals, (4, 2, 1), 0)
-        (mi,) = merge_all(imags, (4, 2, 1), 0)
+            both = sum(eights(ps * coh_ref[q, t, 0]))
+            model_ref[0, 8 * t : 8 * t + 8] = both - sum(eights(pi * coh_ref[q, t, 1]))
+            model_ref[1, 8 * t : 8 * t + 8] = both - sum(eights(pr * coh_ref[q, t, 2]))
+        mr, mi = (sum(model_ref[part, pl.ds(j, times, stride=8), :] for j in range(8)) for part in range(2))
         upper = index * GROUP + lane // TILE - lane % TILE
         differ = meta_ref[0, 3 * n] != meta_ref[0, 3 * n + 1]
         bound = jnp.where(differ, steps * LANES, 0)
-        keep = (upper < bound) & (sample < meta_ref[0, 3 * n + 2])
-        er = jnp.where(keep, vis_ref[n, 0, :, lanes] - mr, 0.0)
-        ei = jnp.where(keep, vis_ref[n, 1, :, lanes] - mi, 0.0)
-        return er, ei
-
-    def gradient(q, errors):
-        er, ei = errors
-        n, index, lanes = where_is(q)
-        acc_re = acc_im = None
+        keep = ((upper < bound) & (sample < meta_ref[0, 3 * n + 2]))[:times]
+        er = jnp.where(keep, vis_ref[q, 0] - mr, 0.0)
+        ei = jnp.where(keep, vis_ref[q, 1] - mi, 0.0)
+        slot = lax.bitwise_and(jnp.int32(q), 1)
+        error_ref[slot, 0, :times] = er + ei
+        error_ref[slot, 1, :times] = ei
+        error_ref[slot, 2, :times] = er
+
+    def gradient(q):
+        n, index = where_is(q)
+        slot = lax.bitwise_and(jnp.int32(q), 1)
+        sums = [None] * 3
         for t in range(times):
-            cr = coh_ref[n, t, 0, :, lanes]
-            ci = coh_ref[n, t, 1, :, lanes]
-            r = jnp.broadcast_to(er[t : t + 1], (k, LANES))
-            i = jnp.broadcast_to(ei[t : t + 1], (k, LANES))
-            re = r * cr + i * ci
-            im = i * cr - r * ci
-            acc_re = re if acc_re is None else acc_re + re
-            acc_im = im if acc_im is None else acc_im + im
-        lr, li = lefts(n, index)
+            for j, c in enumerate((0, 2, 1)):
+                e = error_ref[slot, j, pl.ds(t, 8, stride=0), :]
+                value = [e * part for part in eights(coh_ref[q, t, c])]
+                sums[j] = value if t == 0 else [x + y for x, y in zip(sums[j], value)]
+        both, lone_re, lone_im = (jnp.concatenate(value, axis=0) for value in sums)
+        acc_re = both - lone_re
+        acc_im = both - lone_im
+        lr, li = wide_ref[q, 0], wide_ref[q, 1]
         rr, ri = right_ref[n, 0], right_ref[n, 1]
         second_ref[n, 0] = second_ref[n, 0] + (acc_re * lr + acc_im * li)
         second_ref[n, 1] = second_ref[n, 1] + (acc_re * li - acc_im * lr)
-        parts = eights(acc_re * rr - acc_im * ri) + eights(acc_re * ri + acc_im * rr)
-        (total,) = merge_all(parts, (16, 8, 4), 1)
-        for shift in (2, 1):
-            (total,) = merge_all([total, total], (shift,), 1)
-        first_ref[n, index] = total
-
-    def step(q, errors):
-        following = residual(q + 1)
-        gradient(q, errors)
-        return following
-
-    final = plan.blocks * steps - 1
-    gradient(final, lax.fori_loop(0, final, step, residual(0)))
-
-    results = []
+        terms = jnp.concatenate([acc_re * rr - acc_im * ri, acc_re * ri + acc_im * rr], axis=1)
+        lanes = pl.ds(pl.multiple_of(index * 2 * LANES, 2 * LANES), 2 * LANES)
+        for i, piece in enumerate(pieces(terms, PIECES)):
+            rows = pl.ds(pl.multiple_of((n * PIECES + i) * k, k), k)
+            first_ref[rows, lanes] = piece
+
+    final = plan.total - 1
+
+    def step(q, carry):
+        gradient(q)
+        residual(q + 1)
+        return carry
+
+    residual(0)
+    lax.fori_loop(0, final, step, 0)
+    gradient(final)
+
+    parts = []
     for n in range(plan.blocks):
-        packed = []
-        for base in range(0, steps, 4):
-            value = first_ref[n, base]
-            for r in range(1, 4):
-                value = jnp.where(lane % 4 == r, first_ref[n, base + r], value)
-            packed.append(value)
-        seconds = merge_all(eights(second_ref[n, 0]) + eights(second_ref[n, 1]), (64, 32), 1)
-        part, spot = lane // TILE % 2, lane % TILE
-        rows = []
-        for group in range(k // 8):
-            source = spot % GROUP * TILE + part * 16 + group * 4 + spot // GROUP % 4
-            value = take(packed[0], source)
-            for h in range(1, len(packed)):
-                value = jnp.where(spot // 16 == h, take(packed[h], source), value)
-            other = take(seconds[group % 2], part * 64 + group // 2 * TILE + spot)
-            rows.append(jnp.where(lane < 2 * TILE, value, other))
-        results.append(jnp.concatenate(rows, axis=0))
-    return results
-
-
-def first_kernel(plan, meta_ref, own_ref, sib_ref, vis_ref, coh_ref, out_ref, *scratch):
+        parts += pieces(jnp.concatenate([second_ref[n, 0], second_ref[n, 1]], axis=1), PIECES)
+    value = matmul(jnp.concatenate(parts, axis=0), fold_ref[...])
+    value = value + matmul(first_ref[...], narrow_ref[...])
+    return [
+        sum(value[(n * PIECES + i) * k : (n * PIECES + i + 1) * k] for i in range(PIECES))
+        for n in range(plan.blocks)
+    ]
+
+
+def first_kernel(plan, meta_ref, own_ref, sib_ref, vis_ref, coh_ref, spread_ref, narrow_ref, fold_ref, out_ref, *scratch):
+    fixed = (vis_ref, coh_ref, spread_ref, narrow_ref, fold_ref)
     me = lax.axis_index("pair")
     tile_gains = [
         [plan.fetch(me, own_ref, sib_ref, meta_ref[0, 3 * n + side], 0) for side in range(2)]
         for n in range(plan.blocks)
     ]
-    for n, terms in enumerate(block_gradients(plan, meta_ref, tile_gains, vis_ref, coh_ref, *scratch)):
+    for n, terms in enumerate(block_gradients(plan, meta_ref, tile_gains, *fixed, *scratch)):
         out_ref[n] = terms
 
 
 def second_kernel(
-    plan, step_size, meta_ref, own_ref, sib_ref, term_own_ref, term_sib_ref, mult_ref, vis_ref, coh_ref,
-    part_own_ref, part_sib_ref, rest_ref, *scratch,
+    plan, step_size, meta_ref, own_ref, sib_ref, term_own_ref, term_sib_ref, mult_ref,
+    vis_ref, coh_ref, spread_ref, narrow_ref, fold_ref, part_own_ref, part_sib_ref, rest_ref, *scratch,
 ):
+    fixed = (vis_ref, coh_ref, spread_ref, narrow_ref, fold_ref)
     k = plan.k
     me = lax.axis_index("pair")
     wanted = [meta_ref[0, 3 * n + side] for n in range(plan.blocks) for side in range(2)]
@@ -336,7 +363,7 @@
             sums = gather(slot, sums)
     else:
         sums = lax.fori_loop(0, plan.zn, gather, sums)
-    sums = [s + pltpu.roll(s, LANES // 2, 1) for s in sums]
+    sums = [s + pltpu.roll(s, LANES - TILE, 1) for s in sums]
 
     tile_gains = [
         [
@@ -360,9 +387,9 @@
 
     part_own_ref[...] = jnp.zeros_like(part_own_ref)
     part_sib_ref[...] = jnp.zeros_like(part_sib_ref)
-    for n, terms in enumerate(block_gradients(plan, meta_ref, tile_gains, vis_ref, coh_ref, *scratch)):
+    for n, terms in enumerate(block_gradients(plan, meta_ref, tile_gains, *fixed, *scratch)):
         for side in range(2):
-            plan.spread(me, meta_ref[0, 3 * n + side], terms, side * 2 * TILE, part_own_ref, part_sib_ref)
+            plan.spread(me, meta_ref[0, 3 * n + side], terms, side, part_own_ref, part_sib_ref)
 
 
 def fit_kernel(plan, fit, gain_ref, own_ref, *refs):
@@ -406,9 +433,11 @@
     f32 = lambda *shape: jax.ShapeDtypeStruct(shape, jnp.float32)
     scratch = [
         pltpu.VMEM((blocks, 2, k, LANES), jnp.float32),
-        pltpu.VMEM((blocks, k, LANES), jnp.float32),
+        pltpu.VMEM((plan.total, 2, k, LANES), jnp.float32),
         pltpu.VMEM((blocks, 2, k, LANES), jnp.float32),
-        pltpu.VMEM((blocks, plan.steps, 8, LANES), jnp.float32),
+        pltpu.VMEM((blocks * PIECES * k, 2 * cells), jnp.bfloat16),
+        pltpu.VMEM((2, 8 * times, LANES), jnp.float32),
+        pltpu.VMEM((2, 3, 8, LANES), jnp.float32),
     ]
     params = pltpu.CompilerParams(vmem_limit_bytes=16 << 20)
 
@@ -432,14 +461,28 @@
         name="load",
         in_specs=[hbm] * 2,
         out_specs=[vmem] * 2,
-        out_shape=[f32(blocks, 2, times, cells), f32(blocks, times, 2, k, cells)],
+        out_shape=[f32(plan.total, 2, times, LANES), f32(plan.total, times, 3, k, LANES)],
         scratch_shapes=[
             pltpu.VMEM((blocks, times, 2, cells), jnp.float32),
             pltpu.VMEM((blocks, times, 2, k, cells), jnp.bfloat16),
-            pltpu.SemaphoreType.DMA((2 * blocks + 1,)),
+            pltpu.SemaphoreType.DMA((4 * blocks + 1,)),
         ],
         compiler_params=params,
     )(stay(visibilities), stay(coherencies))
+
+    bf16 = lambda *shape: jax.ShapeDtypeStruct(shape, jnp.bfloat16)
+    tables = pl.pallas_call(
+        lambda *refs: table_kernel(plan, *refs),
+        name="tables",
+        in_specs=[],
+        out_specs=[vmem] * 3,
+        out_shape=[
+            bf16(LANES, 2 * cells),
+            bf16(2 * cells, LANES),
+            bf16(2 * LANES, LANES),
+        ],
+        compiler_params=params,
+    )()
 
     def gather(value):
         parts = [value] + [exchange(value, "pair", pairs, 2 * m) for m in range(1, zn)]
@@ -451,23 +494,23 @@
     terms = pl.pallas_call(
         lambda *refs: first_kernel(plan, *refs),
         name="first",
-        in_specs=[smem, vmem, vmem, vmem, vmem],
+        in_specs=[smem] + [vmem] * 7,
         out_specs=vmem,
         out_shape=f32(blocks, k, LANES),
         scratch_shapes=scratch,
         compiler_params=params,
-    )(meta, own, sib, vis, coh)
+    )(meta, own, sib, vis, coh, *tables)
 
     term_own, term_sib = gather(terms)
     part_own, part_sib, rest = pl.pallas_call(
         lambda *refs: second_kernel(plan, step_size, *refs),
         name="second",
-        in_specs=[smem] + [vmem] * 7,
+        in_specs=[smem] + [vmem] * 10,
         out_specs=[vmem, vmem, vmem],
         out_shape=[f32(zn, k, LANES), f32(zn, k, LANES), f32(2, k, LANES)],
         scratch_shapes=scratch,
         compiler_params=params,
-    )(meta, own, sib, term_own, term_sib, mult_rec, vis, coh)
+    )(meta, own, sib, term_own, term_sib, mult_rec, vis, coh, *tables)
 
     crossed = exchange(part_sib, "pair", pairs, 1)
     total = part_own[0] + crossed[0]

time: 53.2 us -> 44.7 us (0.84)
  Pallas kernels: 18 us -> 9.5 us
    pallas_call x1, Pallas kernels: 7.43 us -> 2.95 us  [local(): pl.pallas_call(lambda *refs: second_kernel(plan, step_size, *refs), name=...]
    pallas_call x1, Pallas kernels: 7.21 us -> 2.86 us  [local(): pl.pallas_call(lambda *refs: first_kernel(plan, *refs), name='first', in_...]
  transfers between devices with their start and end apart: 15 -> 15, of which waited for: 13 -> 13; matrix products, arithmetic and copies ran while one was open for 0% -> 0% of each run, Pallas kernels for 3% -> 5%
where the time goes in v2:
time: 44.7 us; the launch traced here: 44.5 us
  starting transfers between devices  17.7 us (40%)
  waiting for transfers between devices  16.5 us (37%)
  Pallas kernels  9.5 us (21%)
  between operations  0.71 us (2%)
    ppermute x15, starting transfers between devices, exchange(): return lax.ppermute(value, axis, [(i, i ^ mask) for i in range(size)])  17.7 us
    ppermute x15, waiting for transfers between devices, exchange(): return lax.ppermute(value, axis, [(i, i ^ mask) for i in range(size)])  16.5 us
    pallas_call x1, Pallas kernels, local(): pl.pallas_call(lambda *refs: second_kernel(plan, step_size, *refs), name=...  2.95 us
    pallas_call x1, Pallas kernels, local(): pl.pallas_call(lambda *refs: first_kernel(plan, *refs), name='first', in_...  2.86 us
    pallas_call x1, Pallas kernels, local(): pl.pallas_call(lambda *refs: load_kernel(plan, *refs), name='load', in_sp...  1.78 us
    pallas_call x1, Pallas kernels, local(): pl.pallas_call(lambda *refs: pack_kernel(plan, *refs), name='pack', in_sp...  0.96 us
  transfers between devices with their start and end apart: 15, of which 13 were waited for; matrix products, arithmetic and copies ran while one was open for 0% of the time, Pallas kernels for 5%

profile of v2, /device:TPU:0, one launch (start us, length us, event | category | flops | bytes accessed | tf_op | source)
XLA Modules:
  0.0 44.5 jit_solution(11361245712176104617)
XLA Ops:
  0.6 1.0 %pack.1 = (f32[72,128]{1,0:T(8,128)S(1)}, s32[8,128]{1,0:T(8,128)S(1)}, f32[32,128]{1,0:T(8,128)S(1)}) custom-call(s32[2,2]{1,0:T(2,128)} %refs_0_.2, s32[2]{0:T(128)} %refs_1_.2, f32[1,2,32,64]{3,2,1,0:T(8,128)} %refs_2_.1, f32[1,2,32,64]{3,2,1,0:T(8,128)} %refs_3_.1, f32[1,2,32,64]{3,2,1,0:T(8,128)} %refs_4_.1), custom_call_target="tpu_custom_call" | custom-call | tf_op jit(solution)/shard_map/pack/pallas_call | solution.py:444
  1.6 5.1 %collective-permute-start.2 = (f32[72,128]{1,0:T(8,128)S(1)}, f32[72,128]{1,0:T(8,128)S(1)}, u32[]{:S(2)}, u32[]{:S(2)}) collective-permute-start(f32[72,128]{1,0:T(8,128)S(1)} %get-tuple-element.15), channel_id=1, source_target_pairs={{0,6},{1,7},{2,4},{3,5},{4,2},{5,3},{6,0},{7,1},{8,14},{9,15},{10,... | collective-permute-start | bytes 110600 | tf_op jit(solution)/shard_map/ppermute | solution.py:416
  6.7 0.0 collective-permute-start.1
  6.7 0.6 %collective-permute-start = (f32[72,128]{1,0:T(8,128)S(1)}, f32[72,128]{1,0:T(8,128)S(1)}, u32[]{:S(2)}, u32[]{:S(2)}) collective-permute-start(f32[72,128]{1,0:T(8,128)S(1)} %get-tuple-element.15), channel_id=1, source_target_pairs={{0,2},{1,3},{2,0},{3,1},{4,6},{5,7},{6,4},{7,5},{8,10},{9,11},{10,... | collective-permute-start | bytes 110600 | tf_op jit(solution)/shard_map/ppermute | solution.py:416
  7.4 1.3 %collective-permute-done.2 = f32[72,128]{1,0:T(8,128)S(1)} collective-permute-done((f32[72,128]{1,0:T(8,128)S(1)}, f32[72,128]{1,0:T(8,128)S(1)}, u32[]{:S(2)}, u32[]{:S(2)}) %collective-permute-start.2) | collective-permute-done | bytes 36896 | tf_op jit(solution)/shard_map/ppermute | solution.py:416
  8.7 2.9 %collective-permute-done.1 = f32[72,128]{1,0:T(8,128)S(1)} collective-permute-done((f32[72,128]{1,0:T(8,128)S(1)}, f32[72,128]{1,0:T(8,128)S(1)}, u32[]{:S(2)}, u32[]{:S(2)}) %collective-permute-start.1) | collective-permute-done | bytes 36896 | tf_op jit(solution)/shard_map/ppermute | solution.py:416
  11.6 0.0 collective-permute-done
  11.6 0.1 collective-permute-start.3
  11.7 0.2 tables.1
  11.9 1.8 %load.1 = (f32[16,2,8,128]{3,2,1,0:T(8,128)S(1)}, f32[16,8,3,32,128]{4,3,2,1,0:T(8,128)S(1)}) custom-call(f32[1,2,8,2,1024]{4,3,2,1,0:T(2,128)} %refs_0_.3, bf16[1,2,8,2,32,1024]{5,4,3,2,1,0:T(8,128)(2,1)} %refs_1_.3), custom_call_target="tpu_custom_call" | custom-call | tf_op jit(solution)/shard_map/load/pallas_call | solution.py:459
  13.7 0.0 collective-permute-done.3.refs_2_
  13.7 2.9 %first.1 = f32[2,32,128]{2,1,0:T(8,128)S(1)} custom-call(s32[8,128]{1,0:T(8,128)S(1)} %get-tuple-element.14.refs_0_, f32[4,72,128]{2,1,0:T(8,128)S(1)} %pad_maximum_fusion.refs_1_, f32[4,72,128]{2,1,0:T(8,128)S(1)} %collective-permute-done.3.refs_2_, f32[16,2,8,128]{3,2,1,0:T(8,128)S(1)} %get-tuple-element.16.refs_3_.refs_6_, ...), custom_call_target="tpu_custom_call" | custom-call | tf_op jit(solution)/shard_map/first/pallas_call | solution.py:494
  16.6 1.5 %collective-permute-start.6 = (f32[2,32,128]{2,1,0:T(8,128)S(1)}, f32[2,32,128]{2,1,0:T(8,128)S(1)}, u32[]{:S(2)}, u32[]{:S(2)}) collective-permute-start(f32[2,32,128]{2,1,0:T(8,128)S(1)} %first.1), channel_id=1, source_target_pairs={{0,6},{1,7},{2,4},{3,5},{4,2},{5,3},{6,0},{7,1},{8,14},{9,15},{10,... | collective-permute-start | bytes 98312 | tf_op jit(solution)/shard_map/ppermute | solution.py:416
  18.1 0.6 %collective-permute-start.5 = (f32[2,32,128]{2,1,0:T(8,128)S(1)}, f32[2,32,128]{2,1,0:T(8,128)S(1)}, u32[]{:S(2)}, u32[]{:S(2)}) collective-permute-start(f32[2,32,128]{2,1,0:T(8,128)S(1)} %first.1), channel_id=1, source_target_pairs={{0,4},{1,5},{2,6},{3,7},{4,0},{5,1},{6,2},{7,3},{8,12},{9,13},{10,... | collective-permute-start | bytes 98312 | tf_op jit(solution)/shard_map/ppermute | solution.py:416
  18.8 2.3 %collective-permute-start.4 = (f32[2,32,128]{2,1,0:T(8,128)S(1)}, f32[2,32,128]{2,1,0:T(8,128)S(1)}, u32[]{:S(2)}, u32[]{:S(2)}) collective-permute-start(f32[2,32,128]{2,1,0:T(8,128)S(1)} %first.1), channel_id=1, source_target_pairs={{0,2},{1,3},{2,0},{3,1},{4,6},{5,7},{6,4},{7,5},{8,10},{9,11},{10,... | collective-permute-start | bytes 98312 | tf_op jit(solution)/shard_map/ppermute | solution.py:416
  21.1 1.4 %collective-permute-done.6 = f32[2,32,128]{2,1,0:T(8,128)S(1)} collective-permute-done((f32[2,32,128]{2,1,0:T(8,128)S(1)}, f32[2,32,128]{2,1,0:T(8,128)S(1)}, u32[]{:S(2)}, u32[]{:S(2)}) %collective-permute-start.6) | collective-permute-done | bytes 32800 | tf_op jit(solution)/shard_map/ppermute | solution.py:416
  22.4 1.0 %collective-permute-done.5 = f32[2,32,128]{2,1,0:T(8,128)S(1)} collective-permute-done((f32[2,32,128]{2,1,0:T(8,128)S(1)}, f32[2,32,128]{2,1,0:T(8,128)S(1)}, u32[]{:S(2)}, u32[]{:S(2)}) %collective-permute-start.5) | collective-permute-done | bytes 32800 | tf_op jit(solution)/shard_map/ppermute | solution.py:416
  23.5 0.2 collective-permute-done.4
  23.7 0.1 collective-permute-start.7
  23.8 1.3 %collective-permute-done.7.refs_4_ = f32[4,2,32,128]{3,2,1,0:T(8,128)S(1)} collective-permute-done((f32[4,2,32,128]{3,2,1,0:T(8,128)S(1)}, f32[4,2,32,128]{3,2,1,0:T(8,128)S(1)}, u32[]{:S(2)}, u32[]{:S(2)}) %collective-permute-start.7) | collective-permute-done | bytes 131104 | tf_op jit(solution)/shard_map/ppermute | solution.py:416
  25.1 3.0 %second.1 = (f32[4,32,128]{2,1,0:T(8,128)S(1)}, f32[4,32,128]{2,1,0:T(8,128)S(1)}, f32[2,32,128]{2,1,0:T(8,128)S(1)}) custom-call(s32[8,128]{1,0:T(8,128)S(1)} %get-tuple-element.14.refs_0_, f32[4,72,128]{2,1,0:T(8,128)S(1)} %pad_maximum_fusion.refs_1_, f32[4,72,128]{2,1,0:T(8,128)S(1)} %collective-permute-done.3.refs_2_, ...), custom_call_target="tpu_custom_call" | custom-call | tf_op jit(solution)/shard_map/second/pallas_call | solution.py:505
  28.0 0.2 collective-permute-start.8
  28.3 1.1 %collective-permute-done.8 = f32[4,32,128]{2,1,0:T(8,128)S(1)} collective-permute-done((f32[4,32,128]{2,1,0:T(8,128)S(1)}, f32[4,32,128]{2,1,0:T(8,128)S(1)}, u32[]{:S(2)}, u32[]{:S(2)}) %collective-permute-start.8) | collective-permute-done | bytes 65568 | tf_op jit(solution)/shard_map/ppermute | solution.py:416
  29.4 1.4 %collective-permute-start.9 = (f32[32,128]{1,0:T(8,128)S(1)}, f32[32,128]{1,0:T(8,128)S(1)}, u32[]{:S(2)}, u32[]{:S(2)}) collective-permute-start(f32[32,128]{1,0:T(8,128)S(1)} %get-tuple-element.27), channel_id=1, source_target_pairs={{0,2},{1,3},{2,0},{3,1},{4,6},{5,7},{6,4},{7,5},{8,10},{9,11},{10,... | collective-permute-start | bytes 49160 | tf_op jit(solution)/shard_map/ppermute | solution.py:416
  30.8 1.5 %collective-permute-start.11 = (f32[32,128]{1,0:T(8,128)S(1)}, f32[32,128]{1,0:T(8,128)S(1)}, u32[]{:S(2)}, u32[]{:S(2)}) collective-permute-start(f32[32,128]{1,0:T(8,128)S(1)} %get-tuple-element.28), channel_id=1, source_target_pairs={{0,6},{1,7},{2,4},{3,5},{4,2},{5,3},{6,0},{7,1},{8,14},{9,15},{10,... | collective-permute-start | bytes 49160 | tf_op jit(solution)/shard_map/ppermute | solution.py:416
  32.2 0.7 %collective-permute-start.10 = (f32[32,128]{1,0:T(8,128)S(1)}, f32[32,128]{1,0:T(8,128)S(1)}, u32[]{:S(2)}, u32[]{:S(2)}) collective-permute-start(f32[32,128]{1,0:T(8,128)S(1)} %get-tuple-element.29), channel_id=1, source_target_pairs={{0,4},{1,5},{2,6},{3,7},{4,0},{5,1},{6,2},{7,3},{8,12},{9,13},{10,... | collective-permute-start | bytes 49160 | tf_op jit(solution)/shard_map/ppermute | solution.py:416
  32.9 0.2 collective-permute-done.9
  33.2 3.1 %collective-permute-done.11 = f32[32,128]{1,0:T(8,128)S(1)} collective-permute-done((f32[32,128]{1,0:T(8,128)S(1)}, f32[32,128]{1,0:T(8,128)S(1)}, u32[]{:S(2)}, u32[]{:S(2)}) %collective-permute-start.11) | collective-permute-done | bytes 16416 | tf_op jit(solution)/shard_map/ppermute | solution.py:416
  36.3 0.7 %collective-permute-done.10 = f32[32,128]{1,0:T(8,128)S(1)} collective-permute-done((f32[32,128]{1,0:T(8,128)S(1)}, f32[32,128]{1,0:T(8,128)S(1)}, u32[]{:S(2)}, u32[]{:S(2)}) %collective-permute-start.10) | collective-permute-done | bytes 16416 | tf_op jit(solution)/shard_map/ppermute | solution.py:416
  37.0 2.5 %collective-permute-start.14 = (f32[32,128]{1,0:T(8,128)S(1)}, f32[32,128]{1,0:T(8,128)S(1)}, u32[]{:S(2)}, u32[]{:S(2)}) collective-permute-start(f32[32,128]{1,0:T(8,128)S(1)} %get-tuple-element.25.refs_1_), channel_id=1, source_target_pairs={{0,24},{8,16},{16,8},{24,0},{1,25},{9,17},{17,9},{25,1},{2,26},{10... | collective-permute-start | bytes 49160 | tf_op jit(solution)/shard_map/ppermute | solution.py:416
  39.5 0.5 %collective-permute-start.13 = (f32[32,128]{1,0:T(8,128)S(1)}, f32[32,128]{1,0:T(8,128)S(1)}, u32[]{:S(2)}, u32[]{:S(2)}) collective-permute-start(f32[32,128]{1,0:T(8,128)S(1)} %get-tuple-element.25.refs_1_), channel_id=1, source_target_pairs={{0,16},{8,24},{16,0},{24,8},{1,17},{9,25},{17,1},{25,9},{2,18},{10... | collective-permute-start | bytes 49160 | tf_op jit(solution)/shard_map/ppermute | solution.py:416
  40.0 0.5 %collective-permute-start.12 = (f32[32,128]{1,0:T(8,128)S(1)}, f32[32,128]{1,0:T(8,128)S(1)}, u32[]{:S(2)}, u32[]{:S(2)}) collective-permute-start(f32[32,128]{1,0:T(8,128)S(1)} %get-tuple-element.25.refs_1_), channel_id=1, source_target_pairs={{0,8},{8,0},{16,24},{24,16},{1,9},{9,1},{17,25},{25,17},{2,10},{10... | collective-permute-start | bytes 49160 | tf_op jit(solution)/shard_map/ppermute | solution.py:416
  40.6 1.2 %collective-permute-done.14.refs_4_ = f32[32,128]{1,0:T(8,128)S(1)} collective-permute-done((f32[32,128]{1,0:T(8,128)S(1)}, f32[32,128]{1,0:T(8,128)S(1)}, u32[]{:S(2)}, u32[]{:S(2)}) %collective-permute-start.14) | collective-permute-done | bytes 16416 | tf_op jit(solution)/shard_map/ppermute | solution.py:416
  41.8 1.4 %collective-permute-done.13.refs_3_ = f32[32,128]{1,0:T(8,128)S(1)} collective-permute-done((f32[32,128]{1,0:T(8,128)S(1)}, f32[32,128]{1,0:T(8,128)S(1)}, u32[]{:S(2)}, u32[]{:S(2)}) %collective-permute-start.13) | collective-permute-done | bytes 16416 | tf_op jit(solution)/shard_map/ppermute | solution.py:416
  43.3 0.5 %collective-permute-done.12.refs_2_ = f32[32,128]{1,0:T(8,128)S(1)} collective-permute-done((f32[32,128]{1,0:T(8,128)S(1)}, f32[32,128]{1,0:T(8,128)S(1)}, u32[]{:S(2)}, u32[]{:S(2)}) %collective-permute-start.12) | collective-permute-done | bytes 16416 | tf_op jit(solution)/shard_map/ppermute | solution.py:416
  43.8 0.7 %fit.1 = (f32[1,2,32,64]{3,2,1,0:T(8,128)}, f32[1,2,32,64]{3,2,1,0:T(8,128)}, f32[1,2,32,64]{3,2,1,0:T(8,128)}) custom-call(f32[32,128]{1,0:T(8,128)S(1)} %bitcast_add_fusion.1.refs_0_, f32[32,128]{1,0:T(8,128)S(1)} %get-tuple-element.25.refs_1_, f32[32,128]{1,0:T(8,128)S(1)} %collective-permute-done.12.refs_2_, ...), custom_call_target="tpu_custom_call" | custom-call | tf_op jit(solution)/shard_map/fit/pallas_call | solution.py:524
  (5 shorter events, 0.0 us)
Async XLA Ops:
  1.6 7.1 %collective-permute-start.2 = (f32[72,128]{1,0:T(8,128)S(1)}, f32[72,128]{1,0:T(8,128)S(1)}, u32[]{:S(2)}, u32[]{:S(2)}) collective-permute-start(f32[72,128]{1,0:T(8,128)S(1)} %get-tuple-element.15), channel_id=1, source_target_pairs={{0,6},{1,7},{2,4},{3,5},{4,2},{5,3},{6,0},{7,1},{8,14},{9,15},{10,... | collective-permute-start | bytes 110600 | tf_op jit(solution)/shard_map/ppermute | solution.py:416
  6.7 4.9 %collective-permute-start.1 = (f32[72,128]{1,0:T(8,128)S(1)}, f32[72,128]{1,0:T(8,128)S(1)}, u32[]{:S(2)}, u32[]{:S(2)}) collective-permute-start(f32[72,128]{1,0:T(8,128)S(1)} %get-tuple-element.15), channel_id=1, source_target_pairs={{0,4},{1,5},{2,6},{3,7},{4,0},{5,1},{6,2},{7,3},{8,12},{9,13},{10,... | collective-permute-start | bytes 110600 | tf_op jit(solution)/shard_map/ppermute | solution.py:416
  6.7 4.9 %collective-permute-start = (f32[72,128]{1,0:T(8,128)S(1)}, f32[72,128]{1,0:T(8,128)S(1)}, u32[]{:S(2)}, u32[]{:S(2)}) collective-permute-start(f32[72,128]{1,0:T(8,128)S(1)} %get-tuple-element.15), channel_id=1, source_target_pairs={{0,2},{1,3},{2,0},{3,1},{4,6},{5,7},{6,4},{7,5},{8,10},{9,11},{10,... | collective-permute-start | bytes 110600 | tf_op jit(solution)/shard_map/ppermute | solution.py:416
  11.6 2.1 %collective-permute-start.3 = (f32[4,72,128]{2,1,0:T(8,128)S(1)}, f32[4,72,128]{2,1,0:T(8,128)S(1)}, u32[]{:S(2)}, u32[]{:S(2)}) collective-permute-start(f32[4,72,128]{2,1,0:T(8,128)S(1)} %pad_maximum_fusion.refs_1_), channel_id=1, source_target_pairs={{0,1},{1,0},{2,3},{3,2},{4,5},{5,4},{6,7},{7,6},{8,9},{9,8},{10,11... | collective-permute-start | bytes 442376 | tf_op jit(solution)/shard_map/ppermute | solution.py:416
  16.6 5.8 %collective-permute-start.6 = (f32[2,32,128]{2,1,0:T(8,128)S(1)}, f32[2,32,128]{2,1,0:T(8,128)S(1)}, u32[]{:S(2)}, u32[]{:S(2)}) collective-permute-start(f32[2,32,128]{2,1,0:T(8,128)S(1)} %first.1), channel_id=1, source_target_pairs={{0,6},{1,7},{2,4},{3,5},{4,2},{5,3},{6,0},{7,1},{8,14},{9,15},{10,... | collective-permute-start | bytes 98312 | tf_op jit(solution)/shard_map/ppermute | solution.py:416
  18.1 5.3 %collective-permute-start.5 = (f32[2,32,128]{2,1,0:T(8,128)S(1)}, f32[2,32,128]{2,1,0:T(8,128)S(1)}, u32[]{:S(2)}, u32[]{:S(2)}) collective-permute-start(f32[2,32,128]{2,1,0:T(8,128)S(1)} %first.1), channel_id=1, source_target_pairs={{0,4},{1,5},{2,6},{3,7},{4,0},{5,1},{6,2},{7,3},{8,12},{9,13},{10,... | collective-permute-start | bytes 98312 | tf_op jit(solution)/shard_map/ppermute | solution.py:416
  18.8 4.9 %collective-permute-start.4 = (f32[2,32,128]{2,1,0:T(8,128)S(1)}, f32[2,32,128]{2,1,0:T(8,128)S(1)}, u32[]{:S(2)}, u32[]{:S(2)}) collective-permute-start(f32[2,32,128]{2,1,0:T(8,128)S(1)} %first.1), channel_id=1, source_target_pairs={{0,2},{1,3},{2,0},{3,1},{4,6},{5,7},{6,4},{7,5},{8,10},{9,11},{10,... | collective-permute-start | bytes 98312 | tf_op jit(solution)/shard_map/ppermute | solution.py:416
  23.7 1.4 %collective-permute-start.7 = (f32[4,2,32,128]{3,2,1,0:T(8,128)S(1)}, f32[4,2,32,128]{3,2,1,0:T(8,128)S(1)}, u32[]{:S(2)}, u32[]{:S(2)}) collective-permute-start(f32[4,2,32,128]{3,2,1,0:T(8,128)S(1)} %pad_maximum_fusion.1.refs_3_), channel_id=1, source_target_pairs={{0,1},{1,0},{2,3},{3,2},{4,5},{5,4},{6,7},{7,6},{8,9},{9,8},{10,11... | collective-permute-start | bytes 393224 | tf_op jit(solution)/shard_map/ppermute | solution.py:416
  28.0 1.3 %collective-permute-start.8 = (f32[4,32,128]{2,1,0:T(8,128)S(1)}, f32[4,32,128]{2,1,0:T(8,128)S(1)}, u32[]{:S(2)}, u32[]{:S(2)}) collective-permute-start(f32[4,32,128]{2,1,0:T(8,128)S(1)} %get-tuple-element.24), channel_id=1, source_target_pairs={{0,1},{1,0},{2,3},{3,2},{4,5},{5,4},{6,7},{7,6},{8,9},{9,8},{10,11... | collective-permute-start | bytes 196616 | tf_op jit(solution)/shard_map/ppermute | solution.py:416
  29.4 3.8 %collective-permute-start.9 = (f32[32,128]{1,0:T(8,128)S(1)}, f32[32,128]{1,0:T(8,128)S(1)}, u32[]{:S(2)}, u32[]{:S(2)}) collective-permute-start(f32[32,128]{1,0:T(8,128)S(1)} %get-tuple-element.27), channel_id=1, source_target_pairs={{0,2},{1,3},{2,0},{3,1},{4,6},{5,7},{6,4},{7,5},{8,10},{9,11},{10,... | collective-permute-start | bytes 49160 | tf_op jit(solution)/shard_map/ppermute | solution.py:416
  30.8 5.5 %collective-permute-start.11 = (f32[32,128]{1,0:T(8,128)S(1)}, f32[32,128]{1,0:T(8,128)S(1)}, u32[]{:S(2)}, u32[]{:S(2)}) collective-permute-start(f32[32,128]{1,0:T(8,128)S(1)} %get-tuple-element.28), channel_id=1, source_target_pairs={{0,6},{1,7},{2,4},{3,5},{4,2},{5,3},{6,0},{7,1},{8,14},{9,15},{10,... | collective-permute-start | bytes 49160 | tf_op jit(solution)/shard_map/ppermute | solution.py:416
  32.2 4.8 %collective-permute-start.10 = (f32[32,128]{1,0:T(8,128)S(1)}, f32[32,128]{1,0:T(8,128)S(1)}, u32[]{:S(2)}, u32[]{:S(2)}) collective-permute-start(f32[32,128]{1,0:T(8,128)S(1)} %get-tuple-element.29), channel_id=1, source_target_pairs={{0,4},{1,5},{2,6},{3,7},{4,0},{5,1},{6,2},{7,3},{8,12},{9,13},{10,... | collective-permute-start | bytes 49160 | tf_op jit(solution)/shard_map/ppermute | solution.py:416
  37.0 4.8 %collective-permute-start.14 = (f32[32,128]{1,0:T(8,128)S(1)}, f32[32,128]{1,0:T(8,128)S(1)}, u32[]{:S(2)}, u32[]{:S(2)}) collective-permute-start(f32[32,128]{1,0:T(8,128)S(1)} %get-tuple-element.25.refs_1_), channel_id=1, source_target_pairs={{0,24},{8,16},{16,8},{24,0},{1,25},{9,17},{17,9},{25,1},{2,26},{10... | collective-permute-start | bytes 49160 | tf_op jit(solution)/shard_map/ppermute | solution.py:416
  39.5 3.7 %collective-permute-start.13 = (f32[32,128]{1,0:T(8,128)S(1)}, f32[32,128]{1,0:T(8,128)S(1)}, u32[]{:S(2)}, u32[]{:S(2)}) collective-permute-start(f32[32,128]{1,0:T(8,128)S(1)} %get-tuple-element.25.refs_1_), channel_id=1, source_target_pairs={{0,16},{8,24},{16,0},{24,8},{1,17},{9,25},{17,1},{25,9},{2,18},{10... | collective-permute-start | bytes 49160 | tf_op jit(solution)/shard_map/ppermute | solution.py:416
  40.0 3.7 %collective-permute-start.12 = (f32[32,128]{1,0:T(8,128)S(1)}, f32[32,128]{1,0:T(8,128)S(1)}, u32[]{:S(2)}, u32[]{:S(2)}) collective-permute-start(f32[32,128]{1,0:T(8,128)S(1)} %get-tuple-element.25.refs_1_), channel_id=1, source_target_pairs={{0,8},{8,0},{16,24},{24,16},{1,9},{9,1},{17,25},{25,17},{2,10},{10... | collective-permute-start | bytes 49160 | tf_op jit(solution)/shard_map/ppermute | solution.py:416
